TPU v7x, 256 devices: a whole 4x4x8 slice. The times are simulated.
256 devices in a mesh: seq: 64 (over y, z, core), head: 4 (over x).
Axes of the slice: x: 4, y: 4, z: 8, core: 2. Of those that a mesh axis runs over, the one named last changes fastest.
Arguments:
- query_one: bfloat16 [8, 16384, 128], P('head', 'seq'), may hold values from -0.5 to 0.5
- key_one: bfloat16 [8, 16384, 128], P('head', 'seq'), may hold values from -6 to 6
- value_one: bfloat16 [8, 16384, 128], P('head', 'seq'), may hold values from -6 to 6
- decay_one: float32 [8, 16384], P('head', 'seq'), may hold values from -1 to 0
- initial_one: float32 [8, 128, 128], P('head'), may hold values from -768 to 768
- query_two: bfloat16 [8, 16384, 128], P('head', 'seq'), may hold values from -0.5 to 0.5
- key_two: bfloat16 [8, 16384, 128], P('head', 'seq'), may hold values from -6 to 6
- decay_two: float32 [8, 16384], P('head', 'seq'), may hold values from -1 to 0
- initial_two: float32 [8, 128, 128], P('head'), may hold values from -768 to 768
- grad_out: bfloat16 [8, 16384, 128], P('head', 'seq'), may hold values from -6 to 6
Outputs:
- output: bfloat16 [8, 16384, 128], P('head', 'seq')
- grad_query_one: bfloat16 [8, 16384, 128], P('head', 'seq')
- grad_key_one: bfloat16 [8, 16384, 128], P('head', 'seq')
- grad_value_one: bfloat16 [8, 16384, 128], P('head', 'seq')
- grad_query_two: bfloat16 [8, 16384, 128], P('head', 'seq')
- grad_key_two: bfloat16 [8, 16384, 128], P('head', 'seq')
All inputs are finite; a program needn't handle non-finite values.
Results may differ from a plain program's by a relative error of at most 0.015.
Values sent between devices are 32-bit elements; how exact they have to be, the bound alone decides.
No kernel may reach another device: no remote copies, remote signals or barrier semaphores. Data moves between devices by JAX's collectives and lax.ppermute only.
A program may use at most 64 MiB of HBM per device.

v0:
```python
import jax
import jax.numpy as jnp
from jax import lax
from jax.sharding import Mesh
from jax.sharding import PartitionSpec as P

DH = 128
SPAN = 256
SEQ = ("seq_0", "seq_1", "seq_2")


precise_mode = lax.Precision.HIGHEST


def neutral_like(shard, identity):
    return jax.tree.map(
        lambda a, e: jnp.broadcast_to(jnp.asarray(e, a.dtype), a.shape), shard, identity
    )


def entering_2(shard, axes, combine, identity, reverse):
    before = start = neutral_like(shard, identity)
    subtotal = shard
    for axis in reversed(axes):
        size, place = (lax.axis_size(axis), lax.axis_index(axis))
        pieces = jax.tree.map(lambda part: lax.all_gather(part, axis), subtotal)
        inside, subtotal = (start, start)
        for k in reversed(range(size)) if reverse else range(size):
            passed = k > place if reverse else k < place
            subtotal = combine(subtotal, jax.tree.map(lambda part: part[k], pieces))
            inside = jax.tree.map(lambda new, old: jnp.where(passed, new, old), subtotal, inside)
        before = combine(inside, before)
    return before


def from_everyone(shard, axis):
    copies = jnp.broadcast_to(shard, (lax.axis_size(axis), *shard.shape))
    return lax.all_to_all(copies, axis, split_axis=0, concat_axis=0, tiled=True)


def over_copies(shard, axis):
    return from_everyone(shard, axis).sum(axis=0)


def masked_exp(diff, keep_mask):
    return jnp.where(keep_mask, jnp.exp(jnp.where(keep_mask, diff, 0.0)), 0.0)


def decay_sums(log_decay):
    within = jnp.cumsum(log_decay, axis=2)
    block_end = within[:, :, -1]
    upto_end = jnp.cumsum(block_end, axis=1)
    before_end = upto_end - block_end
    return (within, block_end, upto_end, before_end, upto_end[:, -1])


def state_entering(dev_total, device_state, initial):
    heads_local = device_state.shape[0]

    def combine_forward(earlier, later_part):
        return (earlier[0] + later_part[0], jnp.exp(later_part[0]) * earlier[1] + later_part[1])

    identity = (jnp.zeros((heads_local, 1, 1), jnp.float32), jnp.zeros_like(device_state))
    prefix = entering_2(
        (jnp.reshape(dev_total, (heads_local, 1, 1)), device_state),
        SEQ,
        combine_forward,
        identity,
        False,
    )
    return prefix[1] + jnp.exp(prefix[0]) * initial


def grad_leaving(dev_total, device_grad):
    heads_local = device_grad.shape[0]

    def combine_backward(earlier, later_part):
        return (earlier[0] + later_part[0], later_part[1] + jnp.exp(later_part[0]) * earlier[1])

    identity = (jnp.zeros((heads_local, 1, 1), jnp.float32), jnp.zeros_like(device_grad))
    suffix = entering_2(
        (jnp.reshape(dev_total, (heads_local, 1, 1)), device_grad),
        SEQ,
        combine_backward,
        identity,
        True,
    )
    return suffix[1]


def norm_scale(output, head_count):
    squares = over_copies(jnp.sum(output * output, axis=(0, 3)), "head")
    return lax.rsqrt(squares / (head_count * DH) + 1e-06)


def forward_core(queries, keys_block, values, sums, initial):
    within, block_end, upto_end, before_end, dev_total = sums
    span_count = queries.shape[1]
    offsets = jnp.arange(SPAN)
    decay_mask = masked_exp(
        within[:, :, :, None] - within[:, :, None, :],
        (offsets[None, :] <= offsets[:, None])[None, None],
    )
    scores = jnp.einsum("hncd,hnsd->hncs", queries, keys_block, preferred_element_type=jnp.float32)
    weights = (scores * decay_mask).astype(jnp.bfloat16)
    inner_part = jnp.einsum("hncs,hnse->hnce", weights, values, preferred_element_type=jnp.float32)
    keys_scaled = (keys_block * jnp.exp(block_end[:, :, None] - within)[:, :, :, None]).astype(
        jnp.bfloat16
    )
    span_state = jnp.einsum(
        "hncd,hnce->hnde", keys_scaled, values, preferred_element_type=jnp.float32
    )
    device_state = jnp.einsum(
        "hn,hnde->hde", jnp.exp(dev_total[:, None] - upto_end), span_state, precision=precise_mode
    )
    entering = state_entering(dev_total, device_state, initial)
    span_ids = jnp.arange(span_count)
    mixing = masked_exp(
        before_end[:, :, None] - upto_end[:, None, :], (span_ids[None, :] < span_ids[:, None])[None]
    )
    states = jnp.einsum("hji,hide->hjde", mixing, span_state, precision=precise_mode)
    states = states + jnp.exp(before_end)[:, :, None, None] * entering[:, None]
    states_low = states.astype(jnp.bfloat16)
    output = inner_part + jnp.exp(within)[:, :, :, None] * jnp.einsum(
        "hncd,hnde->hnce", queries, states_low, preferred_element_type=jnp.float32
    )
    return (output, weights, decay_mask, states_low)


def backward_core(queries, keys_block, values, sums, saved, grad_in, head_count):
    within, block_end, upto_end, before_end, dev_total = sums
    output, weights, decay_mask, states_low, norm_factor = saved
    span_count = queries.shape[1]
    normalized = output * norm_factor[None, :, :, None]
    cotangent = grad_in.astype(jnp.float32)
    inner_sum = over_copies(jnp.sum(cotangent * normalized, axis=(0, 3)), "head") / (
        head_count * DH
    )
    grad_core = (
        norm_factor[None, :, :, None] * (cotangent - normalized * inner_sum[None, :, :, None])
    ).astype(jnp.bfloat16)
    queries_scaled = (queries * jnp.exp(within)[:, :, :, None]).astype(jnp.bfloat16)
    span_grad = jnp.einsum(
        "hncd,hnce->hnde", queries_scaled, grad_core, preferred_element_type=jnp.float32
    )
    device_grad = jnp.einsum("hn,hnde->hde", jnp.exp(before_end), span_grad, precision=precise_mode)
    leaving = grad_leaving(dev_total, device_grad)
    span_ids = jnp.arange(span_count)
    mixing = masked_exp(
        before_end[:, None, :] - upto_end[:, :, None], (span_ids[None, :] > span_ids[:, None])[None]
    )
    grads_full = jnp.einsum("hji,hide->hjde", mixing, span_grad, precision=precise_mode)
    grads_low = (
        grads_full + jnp.exp(dev_total[:, None] - upto_end)[:, :, None, None] * leaving[:, None]
    ).astype(jnp.bfloat16)
    grad_scores = (
        jnp.einsum("hnce,hnse->hncs", grad_core, values, preferred_element_type=jnp.float32)
        * decay_mask
    ).astype(jnp.bfloat16)
    grad_query = jnp.einsum(
        "hncs,hnsd->hncd", grad_scores, keys_block, preferred_element_type=jnp.float32
    )
    grad_query = grad_query + jnp.exp(within)[:, :, :, None] * jnp.einsum(
        "hnce,hnde->hncd", grad_core, states_low, preferred_element_type=jnp.float32
    )
    tail_weight = jnp.exp(block_end[:, :, None] - within)[:, :, :, None]
    grad_key = jnp.einsum(
        "hncs,hncd->hnsd", grad_scores, queries, preferred_element_type=jnp.float32
    )
    grad_key = grad_key + tail_weight * jnp.einsum(
        "hnse,hnde->hnsd", values, grads_low, preferred_element_type=jnp.float32
    )
    grad_value = jnp.einsum(
        "hncs,hnce->hnse", weights, grad_core, preferred_element_type=jnp.float32
    )
    grad_value = grad_value + tail_weight * jnp.einsum(
        "hnsd,hnde->hnse", keys_block, grads_low, preferred_element_type=jnp.float32
    )
    return (
        grad_query.astype(jnp.bfloat16),
        grad_key.astype(jnp.bfloat16),
        grad_value.astype(jnp.bfloat16),
    )


def local(
    query_one,
    key_one,
    value_one,
    decay_one,
    initial_one,
    query_two,
    key_two,
    decay_two,
    initial_two,
    grad_out,
):
    heads_local = query_one.shape[0]
    head_count = lax.axis_size("head") * heads_local
    tok_rows = query_one.shape[1]
    span_count = tok_rows // SPAN

    def shaped(array):
        return array.reshape(heads_local, span_count, SPAN, DH)

    def flat(array):
        return array.reshape(heads_local, tok_rows, DH)

    sums_one = decay_sums(decay_one.reshape(heads_local, span_count, SPAN))
    sums_two = decay_sums(decay_two.reshape(heads_local, span_count, SPAN))
    queries_one = shaped(query_one)
    keys_one = shaped(key_one)
    values_one = shaped(value_one)
    queries_two = shaped(query_two)
    keys_two = shaped(key_two)
    output_one, weights_one, mask_one, states_one = forward_core(
        queries_one, keys_one, values_one, sums_one, initial_one
    )
    factor_one = norm_scale(output_one, head_count)
    values_two = (output_one * factor_one[None, :, :, None]).astype(jnp.bfloat16)
    output_two, weights_two, mask_two, states_two = forward_core(
        queries_two, keys_two, values_two, sums_two, initial_two
    )
    factor_two = norm_scale(output_two, head_count)
    result = (output_two * factor_two[None, :, :, None]).astype(jnp.bfloat16)
    grads_two = backward_core(
        queries_two,
        keys_two,
        values_two,
        sums_two,
        (output_two, weights_two, mask_two, states_two, factor_two),
        shaped(grad_out),
        head_count,
    )
    grads_one = backward_core(
        queries_one,
        keys_one,
        values_one,
        sums_one,
        (output_one, weights_one, mask_one, states_one, factor_one),
        grads_two[2],
        head_count,
    )
    return (
        flat(result),
        flat(grads_one[0]),
        flat(grads_one[1]),
        flat(grads_one[2]),
        flat(grads_two[0]),
        flat(grads_two[1]),
    )


def solution(mesh):
    finer = Mesh(
        mesh.devices.reshape(4, 8, 2, mesh.shape["head"]), ("seq_0", "seq_1", "seq_2", "head")
    )
    placed = (
        P("head", SEQ, None),
        P("head", SEQ, None),
        P("head", SEQ, None),
        P("head", SEQ),
        P("head", None, None),
        P("head", SEQ, None),
        P("head", SEQ, None),
        P("head", SEQ),
        P("head", None, None),
        P("head", SEQ, None),
    )
    return jax.shard_map(
        local,
        mesh=finer,
        in_specs=placed,
        out_specs=(
            P("head", SEQ, None),
            P("head", SEQ, None),
            P("head", SEQ, None),
            P("head", SEQ, None),
            P("head", SEQ, None),
            P("head", SEQ, None),
        ),
        check_vma=False,
    )
```

profile of v0, /device:TPU:2, one launch (start us, length us, event | category | flops | bytes accessed | tf_op | source)
XLA Modules:
  0.0 284.3 jit_solution(9029784388815044507)
XLA Ops:
  13.4 2.0 all-gather.1
  17.6 2.4 all-reduce.5
  21.3 20.0 %all-reduce.4 = (f32[16]{0:T(128)S(1)}, f32[16]{0:T(128)S(1)}) all-reduce(f32[16]{0:T(128)S(1)} %get-tuple-element.81, f32[16]{0:T(128)S(1)} %get-tuple-element.99), channel_id=8, replica_groups=mesh['seq_0'=4,'seq_1'=8,'seq_2'=2,'head'=4] {'seq_1'}, use_global_device_ids=true, to_apply=%add.1 | all-reduce | flops 32 | bytes 256
  41.4 10.0 %all_gather.94 = f32[4,2,1,1]{1,3,2,0:T(1,128)S(1)} all-gather(f32[1,2,1,1]{1,3,2,0:T(1,128)S(1)} %get-tuple-element.85), channel_id=1, replica_groups=mesh['seq_0'=4,'seq_1'=8,'seq_2'=2,'head'=4] {'seq_0'}, dimensions={0}, use_global_device_ids=true | all-gather | bytes 40 | tf_op jit(solution)/shard_map/all_gather | solution.py:26
  52.2 10.2 %all-gather.13.cloned.1.call-done = f32[8,2,128,128]{3,2,1,0:T(8,128)} async-done(((f32[1,2,128,128]{3,2,1,0:T(8,128)}), f32[8,2,128,128]{3,2,1,0:T(8,128)}) %all-gather.13.cloned.1.call-update) | async-done | bytes 1048592 | tf_op jit(solution)/shard_map/all_gather | solution.py:26
  62.4 1.5 multiply_add_fusion.3
  63.9 13.2 %all_gather.98 = f32[4,2,128,128]{3,2,1,0:T(8,128)S(1)} all-gather(f32[1,2,128,128]{3,2,1,0:T(8,128)S(1)} %multiply_add_fusion.3), channel_id=1, replica_groups=mesh['seq_0'=4,'seq_1'=8,'seq_2'=2,'head'=4] {'seq_0'}, dimensions={0}, use_global_device_ids=true | all-gather | bytes 655360 | tf_op jit(solution)/shard_map/all_gather | solution.py:26
  78.3 4.8 %all-to-all-start = ((f32[4,1,256]{2,1,0:T(1,128)}), f32[4,1,256]{2,1,0:T(1,128)S(1)}, u32[]{:S(2)}, u32[]{:S(2)}) async-start(f32[4,1,256]{2,1,0:T(1,128)} %broadcast_in_dim.124), calls=%async_computation | async-start | bytes 8192 | tf_op jit(solution)/shard_map/all_to_all | solution.py:38
  83.2 3.8 %all-to-all-done = f32[4,1,256]{2,1,0:T(1,128)S(1)} async-done(((f32[4,1,256]{2,1,0:T(1,128)}), f32[4,1,256]{2,1,0:T(1,128)S(1)}, u32[]{:S(2)}, u32[]{:S(2)}) %all-to-all-start) | async-done | bytes 4128 | tf_op jit(solution)/shard_map/all_to_all | solution.py:38
  88.2 2.0 all-gather.3
  91.1 9.5 %all_gather.101 = f32[4,2,1,1]{1,3,2,0:T(1,128)S(1)} all-gather(f32[1,2,1,1]{1,3,2,0:T(1,128)S(1)} %get-tuple-element.103), channel_id=1, replica_groups=mesh['seq_0'=4,'seq_1'=8,'seq_2'=2,'head'=4] {'seq_0'}, dimensions={0}, use_global_device_ids=true | all-gather | bytes 40 | tf_op jit(solution)/shard_map/all_gather | solution.py:26
  101.4 25.3 %all-gather.15.cloned.1.call-done = f32[8,2,128,128]{3,2,1,0:T(8,128)} async-done(((f32[1,2,128,128]{3,2,1,0:T(8,128)}), f32[8,2,128,128]{3,2,1,0:T(8,128)}) %all-gather.15.cloned.1.call-update) | async-done | bytes 1048592 | tf_op jit(solution)/shard_map/all_gather | solution.py:26
  126.7 1.5 multiply_add_fusion.2
  128.2 13.3 %all_gather.105 = f32[4,2,128,128]{3,2,1,0:T(8,128)S(1)} all-gather(f32[1,2,128,128]{3,2,1,0:T(8,128)S(1)} %multiply_add_fusion.2), channel_id=1, replica_groups=mesh['seq_0'=4,'seq_1'=8,'seq_2'=2,'head'=4] {'seq_0'}, dimensions={0}, use_global_device_ids=true | all-gather | bytes 655360 | tf_op jit(solution)/shard_map/all_gather | solution.py:26
  142.7 4.8 %all-to-all-start.1 = ((f32[4,1,256]{2,1,0:T(1,128)}), f32[4,1,256]{2,1,0:T(1,128)S(1)}, u32[]{:S(2)}, u32[]{:S(2)}) async-start(f32[4,1,256]{2,1,0:T(1,128)} %broadcast_in_dim.125), calls=%async_computation.1 | async-start | bytes 8192 | tf_op jit(solution)/shard_map/all_to_all | solution.py:38
  147.6 3.7 %all-to-all-done.1 = f32[4,1,256]{2,1,0:T(1,128)S(1)} async-done(((f32[4,1,256]{2,1,0:T(1,128)}), f32[4,1,256]{2,1,0:T(1,128)S(1)}, u32[]{:S(2)}, u32[]{:S(2)}) %all-to-all-start.1) | async-done | bytes 4128 | tf_op jit(solution)/shard_map/all_to_all | solution.py:38
  151.4 7.6 %all_to_all.20 = f32[4,1,256]{2,1,0:T(1,128)S(1)} all-to-all(f32[4,1,256]{2,1,0:T(1,128)S(1)} %broadcast_in_dim.126), channel_id=1, replica_groups=mesh['seq_0'=4,'seq_1'=8,'seq_2'=2,'head'=4] {'head'}, dimensions={0} | all-to-all | bytes 8192 | tf_op jit(solution)/shard_map/all_to_all | solution.py:38
  159.5 2.0 all-gather.4
  162.2 9.4 %all_gather.110 = f32[4,2,1,1]{1,3,2,0:T(1,128)S(1)} all-gather(f32[1,2,1,1]{1,3,2,0:T(1,128)S(1)} %get-tuple-element.102), channel_id=1, replica_groups=mesh['seq_0'=4,'seq_1'=8,'seq_2'=2,'head'=4] {'seq_0'}, dimensions={0}, use_global_device_ids=true | all-gather | bytes 40 | tf_op jit(solution)/shard_map/all_gather | solution.py:26
  171.6 7.0 %all_gather.115 = f32[4,2,1,1]{1,3,2,0:T(1,128)S(1)} all-gather(f32[1,2,1,1]{1,3,2,0:T(1,128)S(1)} %get-tuple-element.84), channel_id=1, replica_groups=mesh['seq_0'=4,'seq_1'=8,'seq_2'=2,'head'=4] {'seq_0'}, dimensions={0}, use_global_device_ids=true | all-gather | bytes 40 | tf_op jit(solution)/shard_map/all_gather | solution.py:26
  178.9 18.9 %all-gather.17.cloned.1.call-done = f32[8,2,128,128]{3,2,1,0:T(8,128)} async-done(((f32[1,2,128,128]{3,2,1,0:T(8,128)}), f32[8,2,128,128]{3,2,1,0:T(8,128)}) %all-gather.17.cloned.1.call-update) | async-done | bytes 1048592 | tf_op jit(solution)/shard_map/all_gather | solution.py:26
  197.8 1.5 multiply_add_fusion.1
  199.3 13.1 %all_gather.109 = f32[4,2,128,128]{3,2,1,0:T(8,128)S(1)} all-gather(f32[1,2,128,128]{3,2,1,0:T(8,128)S(1)} %multiply_add_fusion.1), channel_id=1, replica_groups=mesh['seq_0'=4,'seq_1'=8,'seq_2'=2,'head'=4] {'seq_0'}, dimensions={0}, use_global_device_ids=true | all-gather | bytes 655360 | tf_op jit(solution)/shard_map/all_gather | solution.py:26
  213.8 4.8 %all-to-all-start.3 = ((f32[4,1,256]{2,1,0:T(1,128)}), f32[4,1,256]{2,1,0:T(1,128)S(1)}, u32[]{:S(2)}, u32[]{:S(2)}) async-start(f32[4,1,256]{2,1,0:T(1,128)} %broadcast_in_dim.127), calls=%async_computation.3 | async-start | bytes 8192 | tf_op jit(solution)/shard_map/all_to_all | solution.py:38
  219.6 2.9 %all-to-all-done.3 = f32[4,1,256]{2,1,0:T(1,128)S(1)} async-done(((f32[4,1,256]{2,1,0:T(1,128)}), f32[4,1,256]{2,1,0:T(1,128)S(1)}, u32[]{:S(2)}, u32[]{:S(2)}) %all-to-all-start.3) | async-done | bytes 4128 | tf_op jit(solution)/shard_map/all_to_all | solution.py:38
  222.8 2.0 all-gather.5
  225.6 0.9 fusion.18
  226.8 0.9 fusion.19
  228.2 0.9 fusion.16
  229.6 31.5 %all-gather.19.cloned.1.call-done = f32[8,2,128,128]{3,2,1,0:T(8,128)} async-done(((f32[1,2,128,128]{3,2,1,0:T(8,128)}), f32[8,2,128,128]{3,2,1,0:T(8,128)}) %all-gather.19.cloned.1.call-update) | async-done | bytes 1048592 | tf_op jit(solution)/shard_map/all_gather | solution.py:26
  261.1 1.5 multiply_add_fusion
  262.6 13.1 %all_gather.114 = f32[4,2,128,128]{3,2,1,0:T(8,128)S(1)} all-gather(f32[1,2,128,128]{3,2,1,0:T(8,128)S(1)} %multiply_add_fusion), channel_id=1, replica_groups=mesh['seq_0'=4,'seq_1'=8,'seq_2'=2,'head'=4] {'seq_0'}, dimensions={0}, use_global_device_ids=true | all-gather | bytes 655360 | tf_op jit(solution)/shard_map/all_gather | solution.py:26
  (138 shorter events, 22.9 us)
Async XLA Ops:
  7.2 5.9 %copy-start = (bf16[2,256,128]{2,1,0:T(8,128)(2,1)S(1)}, bf16[2,256,128]{2,1,0:T(8,128)(2,1)}, u32[]{:S(2)}) copy-start(bf16[2,256,128]{2,1,0:T(8,128)(2,1)} %param.12) | copy-start | bytes 393220
  7.2 0.7 copy-start.12
  7.2 55.2 %all-gather.13.cloned.1.call-start = ((), (), s32[]{:S(2)}) async-start(), calls=%async_computation.4 | async-start | bytes 1179648 | tf_op jit(solution)/shard_map/all_gather | solution.py:26
  8.7 0.7 copy-start.13
  10.8 2.2 copy-start.8
  10.9 0.7 copy-start.15
  15.4 0.7 copy-start.14
  21.0 30.7 %copy-start.7 = (bf16[2,256,128]{2,1,0:T(8,128)(2,1)S(1)}, bf16[2,256,128]{2,1,0:T(8,128)(2,1)}, u32[]{:S(2)}) copy-start(bf16[2,256,128]{2,1,0:T(8,128)(2,1)} %param.10) | copy-start | bytes 393220
  62.4 14.7 %copy-start.3 = (f32[8,2,128,128]{3,2,1,0:T(8,128)S(1)}, f32[8,2,128,128]{3,2,1,0:T(8,128)}, u32[]{:S(2)}) copy-start(f32[8,2,128,128]{3,2,1,0:T(8,128)} %all-gather.13.cloned.1.call-done) | copy-start | bytes 3145732
  63.9 13.2 %copy-start.9 = (f32[2,128,128]{2,1,0:T(8,128)S(1)}, f32[2,128,128]{2,1,0:T(8,128)}, u32[]{:S(2)}) copy-start(f32[2,128,128]{2,1,0:T(8,128)} %param.14) | copy-start | bytes 393220
  78.3 8.6 %all-to-all-start = ((f32[4,1,256]{2,1,0:T(1,128)}), f32[4,1,256]{2,1,0:T(1,128)S(1)}, u32[]{:S(2)}, u32[]{:S(2)}) async-start(f32[4,1,256]{2,1,0:T(1,128)} %broadcast_in_dim.124), calls=%async_computation | async-start | bytes 8192 | tf_op jit(solution)/shard_map/all_to_all | solution.py:38
  83.1 43.6 %all-gather.15.cloned.1.call-start = ((), (), s32[]{:S(2)}) async-start(), calls=%async_computation.5 | async-start | bytes 1179648 | tf_op jit(solution)/shard_map/all_gather | solution.py:26
  87.0 0.9 copy-start.5
  91.0 10.0 %copy-start.6 = (bf16[2,256,128]{2,1,0:T(8,128)(2,1)S(1)}, bf16[2,256,128]{2,1,0:T(8,128)(2,1)}, u32[]{:S(2)}) copy-start(bf16[2,256,128]{2,1,0:T(8,128)(2,1)} %param.15) | copy-start | bytes 393220
  126.7 14.8 %copy-start.4 = (f32[8,2,128,128]{3,2,1,0:T(8,128)S(1)}, f32[8,2,128,128]{3,2,1,0:T(8,128)}, u32[]{:S(2)}) copy-start(f32[8,2,128,128]{3,2,1,0:T(8,128)} %all-gather.15.cloned.1.call-done) | copy-start | bytes 3145732
  128.2 13.3 %copy-start.10 = (f32[2,128,128]{2,1,0:T(8,128)S(1)}, f32[2,128,128]{2,1,0:T(8,128)}, u32[]{:S(2)}) copy-start(f32[2,128,128]{2,1,0:T(8,128)} %param.18) | copy-start | bytes 393220
  141.8 5.7 %copy-start.11 = (bf16[2,256,128]{2,1,0:T(8,128)(2,1)S(1)}, bf16[2,256,128]{2,1,0:T(8,128)(2,1)}, u32[]{:S(2)}) copy-start(bf16[2,256,128]{2,1,0:T(8,128)(2,1)} %param.19) | copy-start | bytes 393220
  142.7 8.6 %all-to-all-start.1 = ((f32[4,1,256]{2,1,0:T(1,128)}), f32[4,1,256]{2,1,0:T(1,128)S(1)}, u32[]{:S(2)}, u32[]{:S(2)}) async-start(f32[4,1,256]{2,1,0:T(1,128)} %broadcast_in_dim.125), calls=%async_computation.1 | async-start | bytes 8192 | tf_op jit(solution)/shard_map/all_to_all | solution.py:38
  147.5 50.3 %all-gather.17.cloned.1.call-start = ((), (), s32[]{:S(2)}) async-start(), calls=%async_computation.6 | async-start | bytes 1179648 | tf_op jit(solution)/shard_map/all_gather | solution.py:26
  197.8 14.6 %copy-start.2 = (f32[8,2,128,128]{3,2,1,0:T(8,128)S(1)}, f32[8,2,128,128]{3,2,1,0:T(8,128)}, u32[]{:S(2)}) copy-start(f32[8,2,128,128]{3,2,1,0:T(8,128)} %all-gather.17.cloned.1.call-done) | copy-start | bytes 3145732
  213.8 8.6 %all-to-all-start.3 = ((f32[4,1,256]{2,1,0:T(1,128)}), f32[4,1,256]{2,1,0:T(1,128)S(1)}, u32[]{:S(2)}, u32[]{:S(2)}) async-start(f32[4,1,256]{2,1,0:T(1,128)} %broadcast_in_dim.127), calls=%async_computation.3 | async-start | bytes 8192 | tf_op jit(solution)/shard_map/all_to_all | solution.py:38
  218.6 42.5 %all-gather.19.cloned.1.call-start = ((), (), s32[]{:S(2)}) async-start(), calls=%async_computation.7 | async-start | bytes 1179648 | tf_op jit(solution)/shard_map/all_gather | solution.py:26
  261.1 14.6 %copy-start.1 = (f32[8,2,128,128]{3,2,1,0:T(8,128)S(1)}, f32[8,2,128,128]{3,2,1,0:T(8,128)}, u32[]{:S(2)}) copy-start(f32[8,2,128,128]{3,2,1,0:T(8,128)} %all-gather.19.cloned.1.call-done) | copy-start | bytes 3145732
Sparse Core Ops, SparseCore 0:
  21.1 41.2 all-gather.12
  91.1 35.5 all-gather.14
  162.4 35.3 all-gather.16
  225.7 35.3 all-gather.18
where the time goes:
time: 285 us; the launch traced here: 284 us
  blocking collectives  127 us (45%)
  waiting for transfers between devices  96.3 us (34%)
  between operations  15.6 us (5%)
  starting transfers between devices  14.4 us (5%)
  other arithmetic  13.2 us (5%)
  matrix products  9.47 us (3%)
  local copies, waits for them, and re-layouts  8.74 us (3%)
    all_gather x12, blocking collectives, entering_2(): pieces = jax.tree.map(lambda part: lax.all_gather(part, axis), subtotal)  96.5 us
    all_gather x4, waiting for transfers between devices, entering_2(): pieces = jax.tree.map(lambda part: lax.all_gather(part, axis), subtotal)  85.9 us
    unnamed x2, blocking collectives  22.4 us
    all_to_all x3, starting transfers between devices, from_everyone(): return lax.all_to_all(copies, axis, split_axis=0, concat_axis=0, tiled=True)  14.4 us
    all_to_all x3, waiting for transfers between devices, from_everyone(): return lax.all_to_all(copies, axis, split_axis=0, concat_axis=0, tiled=True)  10.3 us
    all_to_all x1, blocking collectives, from_everyone(): return lax.all_to_all(copies, axis, split_axis=0, concat_axis=0, tiled=True)  7.64 us
    unnamed x41, local copies, waits for them, and re-layouts  5.78 us
  transfers between devices with their start and end apart: 7, of which 7 were waited for; matrix products, arithmetic and copies ran while one was open for 3% of the time, Pallas kernels for 0%

commit v1 on v0

v1 whole, which is shorter than its diff:
```python
import jax
import jax.numpy as jnp
from jax import lax
from jax.experimental import pallas as pl
from jax.experimental.pallas import tpu as pltpu
from jax.sharding import PartitionSpec as P

DH = 128

exact = lax.Precision.HIGHEST


def head_sum(values):
    size = lax.axis_size("head")
    total = values
    for shift in range(1, size):
        ring = [(i, (i + shift) % size) for i in range(size)]
        total = total + lax.ppermute(values, "head", ring)
    return total


def causal_exp(within):
    tokens = within.shape[1]
    at = jnp.arange(tokens)
    keep = (at[None, :] <= at[:, None])[None]
    diff = within[:, :, None] - within[:, None, :]
    return jnp.where(keep, jnp.exp(jnp.where(keep, diff, 0.0)), 0.0)


def swap(pieces):
    return lax.all_to_all(pieces, "seq", split_axis=0, concat_axis=0, tiled=True)


def round_kernel(full_ref, low_ref):
    low_ref[...] = full_ref[...].astype(low_ref.dtype)


def rounded(full):
    return pl.pallas_call(
        round_kernel,
        out_shape=jax.ShapeDtypeStruct(full.shape, jnp.bfloat16),
        compiler_params=pltpu.CompilerParams(vmem_limit_bytes=4 << 20),
        name="round_state",
    )(full)


def carry_matrix(totals):
    count = totals.shape[0]
    at = jnp.arange(count)
    earlier = at[None, :] < at[:, None]
    between = jnp.dot(
        earlier.astype(jnp.float32),
        jnp.where(earlier, totals[:, None], 0.0),
        precision=exact,
    )
    carry = jnp.where(earlier, jnp.exp(jnp.where(earlier, between, 0.0)), 0.0)
    before = jnp.sum(jnp.where(earlier, totals[None, :], 0.0), axis=1)
    return carry, jnp.exp(before)


def dot_f32(a, b, dims):
    return lax.dot_general(a, b, (dims, ((), ())), precision=exact)


def mm(spec, a, b):
    return jnp.einsum(spec, a, b, preferred_element_type=jnp.float32)


def local(
    query_one,
    key_one,
    value_one,
    decay_one,
    initial_one,
    query_two,
    key_two,
    decay_two,
    initial_two,
    grad_out,
):
    bf16 = jnp.bfloat16
    heads = query_one.shape[0]
    features = lax.axis_size("head") * heads * DH
    seq = lax.axis_size("seq")
    size = heads * DH * DH // seq
    place = lax.axis_index("seq")

    def weights_of(decay):
        within = jnp.cumsum(decay, axis=1)
        end = within[:, -1:]
        return within, jnp.exp(within)[:, :, None], jnp.exp(end - within)[:, :, None], end[:, 0]

    within_one, grow_one, tail_one, end_one = weights_of(decay_one)
    within_two, grow_two, tail_two, end_two = weights_of(decay_two)

    def entering(pieces, carry, start, first):
        return swap(dot_f32(carry, pieces, ((1,), (0,))) + start[:, None] * first[None, :])

    def leaving(pieces, carry):
        return swap(dot_f32(carry, pieces, ((0,), (0,))))

    def spread(state):
        return state.reshape(seq, size)

    def gathered(pieces):
        return rounded(pieces.reshape(heads, DH, DH))

    keys_scaled_one = (key_one * tail_one).astype(bf16)
    span_one = mm("hsd,hse->hde", keys_scaled_one, value_one)
    ends = jnp.stack([end_one, end_two], axis=1)
    ends = jnp.repeat(jnp.pad(ends, ((0, 0), (0, 126))), seq // heads, axis=0)
    got = swap(jnp.concatenate([spread(span_one), ends], axis=1))
    pieces_one, totals = got[:, :size], got[:, size:]
    carry_one, start_one = carry_matrix(totals[:, 0])
    carry_two, start_two = carry_matrix(totals[:, 1])
    first_one = lax.dynamic_index_in_dim(spread(initial_one), place, keepdims=False)
    first_two = lax.dynamic_index_in_dim(spread(initial_two), place, keepdims=False)

    mask_one = causal_exp(within_one)
    weights_one = (mm("hcd,hsd->hcs", query_one, key_one) * mask_one).astype(bf16)
    inner_one = mm("hcs,hse->hce", weights_one, value_one)
    mask_two = causal_exp(within_two)
    weights_two = (mm("hcd,hsd->hcs", query_two, key_two) * mask_two).astype(bf16)

    states_one = gathered(entering(pieces_one, carry_one, start_one, first_one))
    output_one = inner_one + grow_one * mm("hcd,hde->hce", query_one, states_one)
    squares_one = head_sum(jnp.sum(output_one * output_one, axis=(0, 2))[None])[0]
    factor_one = lax.rsqrt(squares_one / features + 1e-06)
    normal_one = output_one * factor_one[None, :, None]
    value_two = normal_one.astype(bf16)

    keys_scaled_two = (key_two * tail_two).astype(bf16)
    span_two = mm("hsd,hse->hde", keys_scaled_two, value_two)
    pieces_two = swap(spread(span_two))
    inner_two = mm("hcs,hse->hce", weights_two, value_two)
    states_two = gathered(entering(pieces_two, carry_two, start_two, first_two))
    output_two = inner_two + grow_two * mm("hcd,hde->hce", query_two, states_two)
    cotangent_two = grad_out.astype(jnp.float32)
    sums = head_sum(
        jnp.stack(
            [
                jnp.sum(output_two * output_two, axis=(0, 2)),
                jnp.sum(output_two * cotangent_two, axis=(0, 2)),
            ]
        )
    )
    factor_two = lax.rsqrt(sums[0] / features + 1e-06)
    inner_sum_two = factor_two * sums[1] / features

    def grad_core_of(cotangent, normalized, factor, inner_sum):
        return (
            factor[None, :, None] * (cotangent - normalized * inner_sum[None, :, None])
        ).astype(bf16)

    normal_two = output_two * factor_two[None, :, None]
    result = normal_two.astype(bf16)

    core_two = grad_core_of(cotangent_two, normal_two, factor_two, inner_sum_two)
    queries_scaled_two = (query_two * grow_two).astype(bf16)
    back_two = swap(spread(mm("hcd,hce->hde", queries_scaled_two, core_two)))
    local_value_two = mm("hcs,hce->hse", weights_two, core_two)
    grads_two = gathered(leaving(back_two, carry_two))
    grad_value_two = (
        local_value_two + tail_two * mm("hsd,hde->hse", key_two, grads_two)
    ).astype(bf16)

    cotangent_one = grad_value_two.astype(jnp.float32)
    inner_sum_one = head_sum(jnp.sum(cotangent_one * normal_one, axis=(0, 2))[None])[0] / features
    core_one = grad_core_of(cotangent_one, normal_one, factor_one, inner_sum_one)
    queries_scaled_one = (query_one * grow_one).astype(bf16)
    back_one = swap(spread(mm("hcd,hce->hde", queries_scaled_one, core_one)))

    def query_grad(core, values, mask, keys, grow, states):
        scores = (mm("hce,hse->hcs", core, values) * mask).astype(bf16)
        grad_query = mm("hcs,hsd->hcd", scores, keys) + grow * mm("hce,hde->hcd", core, states)
        return scores, grad_query.astype(bf16)

    scores_two, grad_query_two = query_grad(
        core_two, value_two, mask_two, key_two, grow_two, states_two
    )
    grad_key_two = (
        mm("hcs,hcd->hsd", scores_two, query_two)
        + tail_two * mm("hse,hde->hsd", value_two, grads_two)
    ).astype(bf16)
    scores_one, grad_query_one = query_grad(
        core_one, value_one, mask_one, key_one, grow_one, states_one
    )
    local_key_one = mm("hcs,hcd->hsd", scores_one, query_one)
    local_value_one = mm("hcs,hce->hse", weights_one, core_one)
    grads_one = gathered(leaving(back_one, carry_one))
    grad_key_one = (
        local_key_one + tail_one * mm("hse,hde->hsd", value_one, grads_one)
    ).astype(bf16)
    grad_value_one = (
        local_value_one + tail_one * mm("hsd,hde->hse", key_one, grads_one)
    ).astype(bf16)
    return result, grad_query_one, grad_key_one, grad_value_one, grad_query_two, grad_key_two


def solution(mesh):
    tokens = P("head", "seq", None)
    decay = P("head", "seq")
    state = P("head", None, None)
    return jax.shard_map(
        local,
        mesh=mesh,
        in_specs=(
            tokens,
            tokens,
            tokens,
            decay,
            state,
            tokens,
            tokens,
            decay,
            state,
            tokens,
        ),
        out_specs=(tokens,) * 6,
        check_vma=False,
    )
```

time: 285 us -> 173 us (0.61)
  the two profiles are of different devices: /device:TPU:2 before, /device:TPU:1 now
where the time goes in v1:
time: 173 us; the launch traced here: 172 us
  waiting for transfers between devices  84.5 us (49%)
  starting transfers between devices  60.9 us (35%)
  matrix products  14 us (8%)
  local copies, waits for them, and re-layouts  9.71 us (6%)
  other arithmetic  2.3 us (1%)
    all_to_all x8, waiting for transfers between devices, swap(): lax.all_to_all(pieces, 'seq', split_axis=0, concat_axis=0, tiled=True)  75.6 us
    all_to_all x8, starting transfers between devices, swap(): lax.all_to_all(pieces, 'seq', split_axis=0, concat_axis=0, tiled=True)  52.8 us
    dot_general x24, matrix products, mm(): return jnp.einsum(spec, a, b, preferred_element_type=jnp.float32)  12.3 us
    ppermute x9, waiting for transfers between devices, head_sum(): total = total + lax.ppermute(values, 'head', ring)  8.88 us
    ppermute x9, starting transfers between devices, head_sum(): total = total + lax.ppermute(values, 'head', ring)  8.07 us
    unnamed x26, local copies, waits for them, and re-layouts  4.28 us
    all_to_all x5, local copies, waits for them, and re-layouts, swap(): lax.all_to_all(pieces, 'seq', split_axis=0, concat_axis=0, tiled=True)  3.94 us
  transfers between devices with their start and end apart: 17, of which 15 were waited for; matrix products, arithmetic and copies ran while one was open for 4% of the time, Pallas kernels for 0%

profile of v1, /device:TPU:1, one launch (start us, length us, event | category | flops | bytes accessed | tf_op | source)
XLA Modules:
  0.0 172.4 jit_solution(6030059553092772514)
XLA Ops:
  4.6 1.2 fusion.32
  6.7 13.3 %all-to-all-start = ((f32[64,1,640]{2,1,0:T(1,128)}), f32[64,1,640]{2,1,0:T(1,128)S(1)}, u32[]{:S(2)}, u32[]{:S(2)}) async-start(f32[64,1,640]{2,1,0:T(1,128)} %all_to_all.56), calls=%async_computation | async-start | bytes 327680 | tf_op jit(solution)/shard_map/all_to_all | solution.py:31
  21.3 9.3 %all-to-all-done = f32[64,1,640]{2,1,0:T(1,128)S(1)} async-done(((f32[64,1,640]{2,1,0:T(1,128)}), f32[64,1,640]{2,1,0:T(1,128)S(1)}, u32[]{:S(2)}, u32[]{:S(2)}) %all-to-all-start) | async-done | bytes 163872 | tf_op jit(solution)/shard_map/all_to_all | solution.py:31
  32.2 5.5 %all-to-all-start.1 = ((f32[64,1,512]{2,1,0:T(1,128)}), f32[64,1,512]{2,1,0:T(1,128)S(1)}, u32[]{:S(2)}, u32[]{:S(2)}) async-start(f32[64,1,512]{2,1,0:T(1,128)} %copy.117), calls=%async_computation.1 | async-start | bytes 262144 | tf_op jit(solution)/shard_map/all_to_all | solution.py:31
  38.0 10.0 %all-to-all-done.1 = f32[64,1,512]{2,1,0:T(1,128)S(1)} async-done(((f32[64,1,512]{2,1,0:T(1,128)}), f32[64,1,512]{2,1,0:T(1,128)S(1)}, u32[]{:S(2)}, u32[]{:S(2)}) %all-to-all-start.1) | async-done | bytes 131104 | tf_op jit(solution)/shard_map/all_to_all | solution.py:31
  48.3 2.5 %collective-permute-start.2 = (f32[1,256]{1,0:T(1,128)S(1)}, f32[1,256]{1,0:T(1,128)S(1)}, u32[]{:S(2)}, u32[]{:S(2)}) collective-permute-start(f32[1,256]{1,0:T(1,128)S(1)} %bitcast.158), channel_id=1, source_target_pairs={{0,3},{1,0},{2,1},{3,2},{4,7},{5,4},{6,5},{7,6},{8,11},{9,8},{10,9... | collective-permute-start | bytes 3080 | tf_op jit(solution)/shard_map/ppermute | solution.py:18
  52.0 2.8 %collective-permute-done.1 = f32[1,256]{1,0:T(1,128)S(1)} collective-permute-done((f32[1,256]{1,0:T(1,128)S(1)}, f32[1,256]{1,0:T(1,128)S(1)}, u32[]{:S(2)}, u32[]{:S(2)}) %collective-permute-start.1) | collective-permute-done | bytes 1056 | tf_op jit(solution)/shard_map/ppermute | solution.py:18
  55.1 0.9 copy-done.1
  55.9 1.0 fusion.33
  56.9 6.6 %all-to-all-start.2 = ((f32[64,1,512]{2,1,0:T(1,128)}), f32[64,1,512]{2,1,0:T(1,128)S(1)}, u32[]{:S(2)}, u32[]{:S(2)}) async-start(f32[64,1,512]{2,1,0:T(1,128)} %bitcast.9), calls=%async_computation.2 | async-start | bytes 262144 | tf_op jit(solution)/shard_map/all_to_all | solution.py:31
  63.9 10.0 %all-to-all-done.2 = f32[64,1,512]{2,1,0:T(1,128)S(1)} async-done(((f32[64,1,512]{2,1,0:T(1,128)}), f32[64,1,512]{2,1,0:T(1,128)S(1)}, u32[]{:S(2)}, u32[]{:S(2)}) %all-to-all-start.2) | async-done | bytes 131104 | tf_op jit(solution)/shard_map/all_to_all | solution.py:31
  74.9 5.0 %all-to-all-start.3 = ((f32[64,1,512]{2,1,0:T(1,128)}), f32[64,1,512]{2,1,0:T(1,128)S(1)}, u32[]{:S(2)}, u32[]{:S(2)}) async-start(f32[64,1,512]{2,1,0:T(1,128)} %copy.122), calls=%async_computation.3 | async-start | bytes 262144 | tf_op jit(solution)/shard_map/all_to_all | solution.py:31
  81.2 9.1 %all-to-all-done.3 = f32[64,1,512]{2,1,0:T(1,128)S(1)} async-done(((f32[64,1,512]{2,1,0:T(1,128)}), f32[64,1,512]{2,1,0:T(1,128)S(1)}, u32[]{:S(2)}, u32[]{:S(2)}) %all-to-all-start.3) | async-done | bytes 131104 | tf_op jit(solution)/shard_map/all_to_all | solution.py:31
  90.7 1.3 collective-permute-start.4
  93.1 1.6 collective-permute-done.4
  94.7 1.2 collective-permute-done.3
  96.0 1.0 fusion.34
  97.0 6.1 %all-to-all-start.4 = ((f32[64,1,512]{2,1,0:T(1,128)}), f32[64,1,512]{2,1,0:T(1,128)S(1)}, u32[]{:S(2)}, u32[]{:S(2)}) async-start(f32[64,1,512]{2,1,0:T(1,128)} %bitcast.18), calls=%async_computation.4 | async-start | bytes 262144 | tf_op jit(solution)/shard_map/all_to_all | solution.py:31
  103.7 9.8 %all-to-all-done.4 = f32[64,1,512]{2,1,0:T(1,128)S(1)} async-done(((f32[64,1,512]{2,1,0:T(1,128)}), f32[64,1,512]{2,1,0:T(1,128)S(1)}, u32[]{:S(2)}, u32[]{:S(2)}) %all-to-all-start.4) | async-done | bytes 131104 | tf_op jit(solution)/shard_map/all_to_all | solution.py:31
  114.6 4.9 %all-to-all-start.5 = ((f32[64,1,512]{2,1,0:T(1,128)}), f32[64,1,512]{2,1,0:T(1,128)S(1)}, u32[]{:S(2)}, u32[]{:S(2)}) async-start(f32[64,1,512]{2,1,0:T(1,128)} %copy.128), calls=%async_computation.5 | async-start | bytes 262144 | tf_op jit(solution)/shard_map/all_to_all | solution.py:31
  119.5 0.9 fusion.18
  121.4 8.4 %all-to-all-done.5 = f32[64,1,512]{2,1,0:T(1,128)S(1)} async-done(((f32[64,1,512]{2,1,0:T(1,128)}), f32[64,1,512]{2,1,0:T(1,128)S(1)}, u32[]{:S(2)}, u32[]{:S(2)}) %all-to-all-start.5) | async-done | bytes 131104 | tf_op jit(solution)/shard_map/all_to_all | solution.py:31
  130.3 1.5 collective-permute-start.8
  132.5 0.9 fusion.19
  133.4 2.3 %collective-permute-done.7 = f32[1,256]{1,0:T(1,128)S(1)} collective-permute-done((f32[1,256]{1,0:T(1,128)S(1)}, f32[1,256]{1,0:T(1,128)S(1)}, u32[]{:S(2)}, u32[]{:S(2)}) %collective-permute-start.7) | collective-permute-done | bytes 1056 | tf_op jit(solution)/shard_map/ppermute | solution.py:18
  136.5 1.0 fusion.35
  137.5 6.6 %all-to-all-start.6 = ((f32[64,1,512]{2,1,0:T(1,128)}), f32[64,1,512]{2,1,0:T(1,128)S(1)}, u32[]{:S(2)}, u32[]{:S(2)}) async-start(f32[64,1,512]{2,1,0:T(1,128)} %bitcast.24), calls=%async_computation.6 | async-start | bytes 262144 | tf_op jit(solution)/shard_map/all_to_all | solution.py:31
  144.5 9.8 %all-to-all-done.6 = f32[64,1,512]{2,1,0:T(1,128)S(1)} async-done(((f32[64,1,512]{2,1,0:T(1,128)}), f32[64,1,512]{2,1,0:T(1,128)S(1)}, u32[]{:S(2)}, u32[]{:S(2)}) %all-to-all-start.6) | async-done | bytes 131104 | tf_op jit(solution)/shard_map/all_to_all | solution.py:31
  155.5 4.9 %all-to-all-start.7 = ((f32[64,1,512]{2,1,0:T(1,128)}), f32[64,1,512]{2,1,0:T(1,128)S(1)}, u32[]{:S(2)}, u32[]{:S(2)}) async-start(f32[64,1,512]{2,1,0:T(1,128)} %copy.136), calls=%async_computation.7 | async-start | bytes 262144 | tf_op jit(solution)/shard_map/all_to_all | solution.py:31
  160.4 0.9 fusion.16
  161.6 9.2 %all-to-all-done.7 = f32[64,1,512]{2,1,0:T(1,128)S(1)} async-done(((f32[64,1,512]{2,1,0:T(1,128)}), f32[64,1,512]{2,1,0:T(1,128)S(1)}, u32[]{:S(2)}, u32[]{:S(2)}) %all-to-all-start.7) | async-done | bytes 131104 | tf_op jit(solution)/shard_map/all_to_all | solution.py:31
  170.7 0.9 fusion.17
  (105 shorter events, 21.0 us)
Async XLA Ops:
  0.6 4.0 %copy-start = (bf16[2,256,128]{2,1,0:T(8,128)(2,1)S(1)}, bf16[2,256,128]{2,1,0:T(8,128)(2,1)}, u32[]{:S(2)}) copy-start(bf16[2,256,128]{2,1,0:T(8,128)(2,1)} %param.12) | copy-start | bytes 393220
  2.4 0.7 copy-start.8
  6.7 13.3 %copy-start.5 = (f32[2,128,128]{2,1,0:T(8,128)S(1)}, f32[2,128,128]{2,1,0:T(8,128)}, u32[]{:S(2)}) copy-start(f32[2,128,128]{2,1,0:T(8,128)} %param.14) | copy-start | bytes 393220
  6.7 23.9 %all-to-all-start = ((f32[64,1,640]{2,1,0:T(1,128)}), f32[64,1,640]{2,1,0:T(1,128)S(1)}, u32[]{:S(2)}, u32[]{:S(2)}) async-start(f32[64,1,640]{2,1,0:T(1,128)} %all_to_all.56), calls=%async_computation | async-start | bytes 327680 | tf_op jit(solution)/shard_map/all_to_all | solution.py:31
  20.1 0.9 copy-start.3
  20.1 1.0 copy-start.4
  32.2 5.5 %copy-start.6 = (f32[2,128,128]{2,1,0:T(8,128)S(1)}, f32[2,128,128]{2,1,0:T(8,128)}, u32[]{:S(2)}) copy-start(f32[2,128,128]{2,1,0:T(8,128)} %param.18) | copy-start | bytes 393220
  32.2 15.8 %all-to-all-start.1 = ((f32[64,1,512]{2,1,0:T(1,128)}), f32[64,1,512]{2,1,0:T(1,128)S(1)}, u32[]{:S(2)}, u32[]{:S(2)}) async-start(f32[64,1,512]{2,1,0:T(1,128)} %copy.117), calls=%async_computation.1 | async-start | bytes 262144 | tf_op jit(solution)/shard_map/all_to_all | solution.py:31
  48.3 3.7 %collective-permute-start.2 = (f32[1,256]{1,0:T(1,128)S(1)}, f32[1,256]{1,0:T(1,128)S(1)}, u32[]{:S(2)}, u32[]{:S(2)}) collective-permute-start(f32[1,256]{1,0:T(1,128)S(1)} %bitcast.158), channel_id=1, source_target_pairs={{0,3},{1,0},{2,1},{3,2},{4,7},{5,4},{6,5},{7,6},{8,11},{9,8},{10,9... | collective-permute-start | bytes 3080 | tf_op jit(solution)/shard_map/ppermute | solution.py:18
  50.9 3.9 %collective-permute-start.1 = (f32[1,256]{1,0:T(1,128)S(1)}, f32[1,256]{1,0:T(1,128)S(1)}, u32[]{:S(2)}, u32[]{:S(2)}) collective-permute-start(f32[1,256]{1,0:T(1,128)S(1)} %bitcast.159), channel_id=1, source_target_pairs={{0,2},{1,3},{2,0},{3,1},{4,6},{5,7},{6,4},{7,5},{8,10},{9,11},{10,... | collective-permute-start | bytes 3080 | tf_op jit(solution)/shard_map/ppermute | solution.py:18
  51.4 3.6 %collective-permute-start = (f32[1,256]{1,0:T(1,128)S(1)}, f32[1,256]{1,0:T(1,128)S(1)}, u32[]{:S(2)}, u32[]{:S(2)}) collective-permute-start(f32[1,256]{1,0:T(1,128)S(1)} %bitcast.160), channel_id=1, source_target_pairs={{0,1},{1,2},{2,3},{3,0},{4,5},{5,6},{6,7},{7,4},{8,9},{9,10},{10,1... | collective-permute-start | bytes 3080 | tf_op jit(solution)/shard_map/ppermute | solution.py:18
  55.0 0.9 copy-start.1
  56.9 16.9 %all-to-all-start.2 = ((f32[64,1,512]{2,1,0:T(1,128)}), f32[64,1,512]{2,1,0:T(1,128)S(1)}, u32[]{:S(2)}, u32[]{:S(2)}) async-start(f32[64,1,512]{2,1,0:T(1,128)} %bitcast.9), calls=%async_computation.2 | async-start | bytes 262144 | tf_op jit(solution)/shard_map/all_to_all | solution.py:31
  74.9 5.0 %copy-start.2 = (bf16[2,256,128]{2,1,0:T(8,128)(2,1)S(1)}, bf16[2,256,128]{2,1,0:T(8,128)(2,1)}, u32[]{:S(2)}) copy-start(bf16[2,256,128]{2,1,0:T(8,128)(2,1)} %param.15) | copy-start | bytes 393220
  74.9 15.4 %all-to-all-start.3 = ((f32[64,1,512]{2,1,0:T(1,128)}), f32[64,1,512]{2,1,0:T(1,128)S(1)}, u32[]{:S(2)}, u32[]{:S(2)}) async-start(f32[64,1,512]{2,1,0:T(1,128)} %copy.122), calls=%async_computation.3 | async-start | bytes 262144 | tf_op jit(solution)/shard_map/all_to_all | solution.py:31
  79.9 0.9 copy-start.7
  90.6 2.5 %collective-permute-start.5 = (f32[2,256]{1,0:T(2,128)S(1)}, f32[2,256]{1,0:T(2,128)S(1)}, u32[]{:S(2)}, u32[]{:S(2)}) collective-permute-start(f32[2,256]{1,0:T(2,128)S(1)} %pad_maximum_fusion.1), channel_id=1, source_target_pairs={{0,3},{1,0},{2,1},{3,2},{4,7},{5,4},{6,5},{7,6},{8,11},{9,8},{10,9... | collective-permute-start | bytes 6152 | tf_op jit(solution)/shard_map/ppermute | solution.py:18
  90.7 4.0 %collective-permute-start.4 = (f32[2,256]{1,0:T(2,128)S(1)}, f32[2,256]{1,0:T(2,128)S(1)}, u32[]{:S(2)}, u32[]{:S(2)}) collective-permute-start(f32[2,256]{1,0:T(2,128)S(1)} %pad_maximum_fusion.1), channel_id=1, source_target_pairs={{0,2},{1,3},{2,0},{3,1},{4,6},{5,7},{6,4},{7,5},{8,10},{9,11},{10,... | collective-permute-start | bytes 6152 | tf_op jit(solution)/shard_map/ppermute | solution.py:18
  92.0 3.9 %collective-permute-start.3 = (f32[2,256]{1,0:T(2,128)S(1)}, f32[2,256]{1,0:T(2,128)S(1)}, u32[]{:S(2)}, u32[]{:S(2)}) collective-permute-start(f32[2,256]{1,0:T(2,128)S(1)} %pad_maximum_fusion.1), channel_id=1, source_target_pairs={{0,1},{1,2},{2,3},{3,0},{4,5},{5,6},{6,7},{7,4},{8,9},{9,10},{10,1... | collective-permute-start | bytes 6152 | tf_op jit(solution)/shard_map/ppermute | solution.py:18
  97.0 16.5 %all-to-all-start.4 = ((f32[64,1,512]{2,1,0:T(1,128)}), f32[64,1,512]{2,1,0:T(1,128)S(1)}, u32[]{:S(2)}, u32[]{:S(2)}) async-start(f32[64,1,512]{2,1,0:T(1,128)} %bitcast.18), calls=%async_computation.4 | async-start | bytes 262144 | tf_op jit(solution)/shard_map/all_to_all | solution.py:31
  114.6 15.2 %all-to-all-start.5 = ((f32[64,1,512]{2,1,0:T(1,128)}), f32[64,1,512]{2,1,0:T(1,128)S(1)}, u32[]{:S(2)}, u32[]{:S(2)}) async-start(f32[64,1,512]{2,1,0:T(1,128)} %copy.128), calls=%async_computation.5 | async-start | bytes 262144 | tf_op jit(solution)/shard_map/all_to_all | solution.py:31
  130.3 3.1 %collective-permute-start.8 = (f32[1,256]{1,0:T(1,128)S(1)}, f32[1,256]{1,0:T(1,128)S(1)}, u32[]{:S(2)}, u32[]{:S(2)}) collective-permute-start(f32[1,256]{1,0:T(1,128)S(1)} %bitcast.154), channel_id=1, source_target_pairs={{0,3},{1,0},{2,1},{3,2},{4,7},{5,4},{6,5},{7,6},{8,11},{9,8},{10,9... | collective-permute-start | bytes 3080 | tf_op jit(solution)/shard_map/ppermute | solution.py:18
  131.9 3.9 %collective-permute-start.7 = (f32[1,256]{1,0:T(1,128)S(1)}, f32[1,256]{1,0:T(1,128)S(1)}, u32[]{:S(2)}, u32[]{:S(2)}) collective-permute-start(f32[1,256]{1,0:T(1,128)S(1)} %bitcast.155), channel_id=1, source_target_pairs={{0,2},{1,3},{2,0},{3,1},{4,6},{5,7},{6,4},{7,5},{8,10},{9,11},{10,... | collective-permute-start | bytes 3080 | tf_op jit(solution)/shard_map/ppermute | solution.py:18
  132.5 3.6 %collective-permute-start.6 = (f32[1,256]{1,0:T(1,128)S(1)}, f32[1,256]{1,0:T(1,128)S(1)}, u32[]{:S(2)}, u32[]{:S(2)}) collective-permute-start(f32[1,256]{1,0:T(1,128)S(1)} %bitcast.156), channel_id=1, source_target_pairs={{0,1},{1,2},{2,3},{3,0},{4,5},{5,6},{6,7},{7,4},{8,9},{9,10},{10,1... | collective-permute-start | bytes 3080 | tf_op jit(solution)/shard_map/ppermute | solution.py:18
  137.5 16.9 %all-to-all-start.6 = ((f32[64,1,512]{2,1,0:T(1,128)}), f32[64,1,512]{2,1,0:T(1,128)S(1)}, u32[]{:S(2)}, u32[]{:S(2)}) async-start(f32[64,1,512]{2,1,0:T(1,128)} %bitcast.24), calls=%async_computation.6 | async-start | bytes 262144 | tf_op jit(solution)/shard_map/all_to_all | solution.py:31
  155.5 15.2 %all-to-all-start.7 = ((f32[64,1,512]{2,1,0:T(1,128)}), f32[64,1,512]{2,1,0:T(1,128)S(1)}, u32[]{:S(2)}, u32[]{:S(2)}) async-start(f32[64,1,512]{2,1,0:T(1,128)} %copy.136), calls=%async_computation.7 | async-start | bytes 262144 | tf_op jit(solution)/shard_map/all_to_all | solution.py:31

commit v2 on v1

v2 whole, which is shorter than its diff:
```python
import functools

import jax
import jax.numpy as jnp
from jax import lax
from jax.experimental import pallas as pl
from jax.experimental.pallas import tpu as pltpu
from jax.sharding import Mesh
from jax.sharding import PartitionSpec as P

DH = 128


def head_sum(values):
    total = values
    for pairs in (((0, 1), (2, 3)), ((1, 2), (3, 0))):
        both = [p for a, b in pairs for p in ((a, b), (b, a))]
        total = total + lax.ppermute(total, "head", both)
    return total


def causal_exp(within):
    tokens = within.shape[1]
    at = jnp.arange(tokens)
    keep = (at[None, :] <= at[:, None])[None]
    diff = within[:, :, None] - within[:, None, :]
    return jnp.where(keep, jnp.exp(jnp.where(keep, diff, 0.0)), 0.0)


def swap(pieces):
    return lax.all_to_all(pieces, "chip", split_axis=0, concat_axis=0, tiled=True)


def pair_swap(values):
    return lax.ppermute(values, "core", ((0, 1), (1, 0)))


def call(kernel, out_shape, *args, place=None, after=(), space=pltpu.VMEM, limit=16 << 20, **more):
    specs = [pl.BlockSpec(memory_space=space)] * len(args)
    if place is not None:
        specs.insert(0, pl.BlockSpec(memory_space=pltpu.SMEM))
        args = (place,) + args
    if after:
        inner, first, last = kernel, len(args), len(args) + len(after)
        specs += [pl.BlockSpec(memory_space=pl.ANY)] * len(after)
        args += tuple(after)

        def kernel(*refs):
            inner(*refs[:first], *refs[last:])

    return pl.pallas_call(
        kernel,
        out_shape=out_shape,
        in_specs=specs,
        compiler_params=pltpu.CompilerParams(vmem_limit_bytes=limit),
        **more,
    )(*args)


def iota(shape, dim):
    return lax.broadcasted_iota(jnp.int32, shape, dim)


def kdot(a, b, dims=((1,), (0,))):
    return lax.dot_general(a, b, (dims, ((), ())), preferred_element_type=jnp.float32)


def two_parts(full):
    high = full.astype(jnp.bfloat16)
    return high, (full - high.astype(jnp.float32)).astype(jnp.bfloat16)


def carried(high, low, pieces):
    first, second = two_parts(pieces)
    both = kdot(high, jnp.concatenate([first, second], axis=1))
    return both[:, :DH] + both[:, DH:] + kdot(low, first)


def decay_matrix(totals, step, forward):
    count = totals.shape[0]
    one = totals.astype(jnp.bfloat16).astype(jnp.float32)
    rest = totals - one
    two = rest.astype(jnp.bfloat16).astype(jnp.float32)
    parts = jnp.concatenate([one, two, rest - two, jnp.zeros_like(one)], axis=0)
    rows, inner, columns = 4 * count, 4 * count, step * count
    at, middle = iota((rows, inner), 0) // 4, iota((rows, inner), 1) % count
    left = middle < at if forward else middle > at
    middle, of = iota((inner, columns), 0) % count, iota((inner, columns), 1) // step
    right = middle > of if forward else middle < of
    between = kdot(
        jnp.where(left, 1.0, 0.0).astype(jnp.bfloat16),
        jnp.where(right, parts, 0.0).astype(jnp.bfloat16),
    )
    row, column = iota((rows, columns), 0), iota((rows, columns), 1)
    order = column // step < row // 4 if forward else column // step > row // 4
    keep = order & (column % step == row % 4)
    return jnp.where(keep, jnp.exp(jnp.where(keep, between, 0.0)), 0.0)


def lane_of(row, lane):
    return jnp.sum(jnp.where(iota(row.shape, 1) == lane, row, 0.0), axis=1, keepdims=True)


def first_span_kernel(
    core_ref, key_hbm, value_hbm, one_hbm, two_hbm, mine_ref, send_ref, key_ref, value_ref, one_ref, two_ref, state, sems
):
    arrays = ((one_hbm, one_ref), (two_hbm, two_ref), (key_hbm, key_ref), (value_hbm, value_ref))
    copies = [pltpu.make_async_copy(a, b, sems.at[i]) for i, (a, b) in enumerate(arrays)]
    for copy in copies:
        copy.start()
    for copy in copies:
        copy.wait()
    heads, tokens, _ = key_ref.shape
    lane = iota((1, DH), 1)
    ends = jnp.zeros((1, DH), jnp.float32)
    later = iota((tokens, tokens), 1) > iota((tokens, tokens), 0)
    for h in range(heads):
        decay = one_ref[h : h + 1, :]
        after = jnp.sum(jnp.where(later, decay, 0.0), axis=1, keepdims=True)
        scaled = (key_ref[h].astype(jnp.float32) * jnp.exp(after)).astype(jnp.bfloat16)
        state[h] = kdot(scaled, value_ref[h], ((0,), (0,)))
        end_one = jnp.sum(decay, axis=1, keepdims=True)
        end_two = jnp.sum(two_ref[h : h + 1, :], axis=1, keepdims=True)
        ends = jnp.where(lane == h, end_one, jnp.where(lane == heads + h, end_two, ends))
    core = core_ref[0]
    for ref, head in ((mine_ref, core), (send_ref, 1 - core)):
        ref[:DH, :] = state[head]
        ref[DH:, :] = jnp.broadcast_to(ends, (8, DH))


def first_merge_kernel(core_ref, mine_ref, got_ref, sent_ref, ends_ref, total):
    core = core_ref[0]
    heads = 2
    lower = core == 0
    own, other = mine_ref[DH : DH + 1, :], got_ref[DH : DH + 1, :]
    first = jnp.where(lower, own, other)
    second = jnp.where(lower, other, own)
    ends = [lane_of(row, n + core) for n in (0, heads) for row in (first, second)]
    grown = jnp.exp(ends[1])
    total[...] = mine_ref[:DH, :] * jnp.where(lower, grown, 1.0) + got_ref[:DH, :] * jnp.where(
        lower, 1.0, grown
    )
    lane = iota((1, DH), 1)
    row = jnp.where(lane == 0, ends[0] + ends[1], jnp.where(lane == 1, ends[2] + ends[3], 0.0))
    count = sent_ref.shape[0] // 8
    sent_ref[...] = jnp.where(iota(sent_ref.shape, 0) % 8 == 4, row, 0.0)
    for q in range(4):
        sent_ref[pl.ds(q, count, stride=8), :] = total[pl.ds(q, count, stride=4), :]
    for i in range(4):
        ends_ref[i : i + 1, :] = jnp.broadcast_to(jnp.exp(ends[i]), (1, DH))
    ends_ref[4:, :] = jnp.zeros((4, DH), jnp.float32)


def chip_totals(got_ref):
    return got_ref[pl.ds(4, got_ref.shape[0] // 8, stride=8), :]


def first_scan_kernel(place_ref, got_ref, out_ref, start_ref, *matrix_refs):
    ends = chip_totals(got_ref)
    one, two = lane_of(ends, 0), lane_of(ends, 1)
    out_ref[...] = carried(*two_parts(decay_matrix(one, 8, True)), got_ref[...])
    for i, (totals, forward) in enumerate(((two, True), (two, False), (one, False))):
        matrix_refs[2 * i][...], matrix_refs[2 * i + 1][...] = two_parts(
            decay_matrix(totals, 4, forward)
        )
    earlier = iota(ends.shape, 0) < place_ref[0]
    before = jnp.exp(jnp.sum(jnp.where(earlier, ends, 0.0), axis=0, keepdims=True))
    for i in range(2):
        start_ref[i : i + 1, :] = jnp.broadcast_to(lane_of(before, i), (1, DH))
    start_ref[2:, :] = jnp.zeros((6, DH), jnp.float32)


def scan_kernel(high_ref, low_ref, got_ref, out_ref):
    out_ref[...] = carried(high_ref[...], low_ref[...], got_ref[...])


def place_kernel(core_ref, keep_ref, got_ref, out_ref):
    core = core_ref[0]
    out_ref[core] = keep_ref[...].astype(out_ref.dtype)
    out_ref[1 - core] = got_ref[...].astype(out_ref.dtype)


def split_kernel(core_ref, span_ref, mine_ref, send_ref):
    core = core_ref[0]
    mine_ref[...] = span_ref[core]
    send_ref[...] = span_ref[1 - core]


def merge_kernel(row, forward, core_ref, mine_ref, got_ref, grown_ref, total_ref):
    mine_decays = core_ref[0] == (0 if forward else 1)
    grown = grown_ref[row : row + 1, :]
    total_ref[...] = mine_ref[...] * jnp.where(mine_decays, grown, 1.0) + got_ref[
        ...
    ] * jnp.where(mine_decays, 1.0, grown)


def enter_kernel(
    row, core_ref, state_ref, mine_ref, got_ref, grown_ref, start_ref, initial_ref, keep_ref, send_ref
):
    core = core_ref[0]
    lower = core == 0
    start, grown = start_ref[row : row + 1, :], grown_ref[2 * row : 2 * row + 1, :]
    first = state_ref[...] + start * initial_ref[...]
    second = grown * first + jnp.where(lower, mine_ref[:DH, :], got_ref[:DH, :])
    keep_ref[...] = jnp.where(lower, first, second)
    send_ref[...] = jnp.where(lower, second, first)


def leave_kernel(row, core_ref, grad_ref, mine_ref, got_ref, grown_ref, keep_ref, send_ref):
    lower = core_ref[0] == 0
    second = grad_ref[...]
    first = grown_ref[row : row + 1, :] * second + jnp.where(lower, got_ref[...], mine_ref[...])
    keep_ref[...] = jnp.where(lower, first, second)
    send_ref[...] = jnp.where(lower, second, first)


def copy_kernel(*refs):
    half = len(refs) // 2
    for a, b in zip(refs[:half], refs[half:]):
        b[...] = a[...]


def pick_kernel(core_ref, *refs):
    half = len(refs) // 2
    for a, b in zip(refs[:half], refs[half:]):
        b[...] = a[core_ref[0]]


def last_kernel(
    core_ref, keep_ref, got_ref, key_ref, value_ref, tail_ref, local_key_ref, local_value_ref, grad_key_ref, grad_value_ref
):
    core = core_ref[0]
    for head, ref in ((core, keep_ref), (1 - core, got_ref)):
        grads = ref[...].astype(jnp.bfloat16)
        tail = tail_ref[head]
        grad_key = local_key_ref[head] + tail * kdot(value_ref[head], grads, ((1,), (1,)))
        grad_value = local_value_ref[head] + tail * kdot(key_ref[head], grads)
        grad_key_ref[head] = grad_key.astype(grad_key_ref.dtype)
        grad_value_ref[head] = grad_value.astype(grad_value_ref.dtype)


def decay_kernel(one_ref, two_ref, grad_ref, within_one_ref, within_two_ref, late_grad_ref):
    late_grad_ref[...] = grad_ref[...]
    decay = jnp.concatenate([one_ref[...], two_ref[...]], axis=0)
    first = decay.astype(jnp.bfloat16).astype(jnp.float32)
    rest = decay - first
    second = rest.astype(jnp.bfloat16).astype(jnp.float32)
    zero = jnp.zeros_like(first)
    parts = jnp.concatenate([first, second, rest - second, zero], axis=0).astype(jnp.bfloat16)
    tokens = decay.shape[1]
    upto = iota((tokens, tokens), 0) <= iota((tokens, tokens), 1)
    sums = kdot(parts, jnp.where(upto, 1.0, 0.0).astype(jnp.bfloat16))
    within = (sums[8:12] + sums[4:8]) + sums[:4]
    within_one_ref[...] = within[:2]
    within_two_ref[...] = within[2:]


def later(after, *arrays):
    out = call(
        copy_kernel,
        tuple(jax.ShapeDtypeStruct(a.shape, a.dtype) for a in arrays),
        *arrays,
        after=(after,),
    )
    return out if len(arrays) > 1 else out[0]


def mm(spec, a, b):
    return jnp.einsum(spec, a, b, preferred_element_type=jnp.float32)


def local(
    query_one,
    key_one,
    value_one,
    decay_one,
    initial_one,
    query_two,
    key_two,
    decay_two,
    initial_two,
    grad_out,
):
    bf16 = jnp.bfloat16
    heads = query_one.shape[0]
    features = lax.axis_size("head") * heads * DH
    chips = lax.axis_size("chip")
    tokens = query_one.shape[1]
    place = lax.axis_index("chip").reshape(1)
    core = lax.axis_index("core").reshape(1)
    f32 = jnp.float32
    flat = jax.ShapeDtypeStruct((DH, DH), f32)

    def exchanged(state):
        return swap(state.reshape(chips, -1, DH)).reshape(-1, DH)

    def placed(keep, send):
        low = jax.ShapeDtypeStruct((heads, DH, DH), bf16)
        return call(place_kernel, low, keep, pair_swap(send), place=core)

    def halves(span):
        mine, send = call(split_kernel, (flat,) * 2, span, place=core)
        return mine, pair_swap(send)

    def merged(row, forward, mine, got):
        kernel = functools.partial(merge_kernel, row, forward)
        return call(kernel, flat, mine, got, grown, place=core)

    def scanned(matrix, total):
        return exchanged(call(scan_kernel, flat, *matrix, exchanged(total)))

    def entering(row, state, mine, got, initial):
        kernel = functools.partial(enter_kernel, row)
        args = (state, mine, got, grown, start, initial)
        return placed(*call(kernel, (flat,) * 2, *args, place=core))

    def left(row, grad, mine, got):
        kernel = functools.partial(leave_kernel, row)
        return call(kernel, (flat,) * 2, grad, mine, got, grown, place=core)

    def grow_tail(within, end):
        return jnp.exp(within)[:, :, None], jnp.exp(end - within)[:, :, None]

    mine_one, send = call(
        first_span_kernel,
        (jax.ShapeDtypeStruct((DH + 8, DH), f32),) * 2,
        key_one,
        value_one,
        decay_one,
        decay_two,
        place=core,
        space=pltpu.HBM,
        limit=62 << 20,
        scratch_shapes=[
            pltpu.VMEM((heads, tokens, DH), bf16),
            pltpu.VMEM((heads, tokens, DH), bf16),
            pltpu.VMEM((heads, tokens), f32),
            pltpu.VMEM((heads, tokens), f32),
            pltpu.VMEM((heads, DH, DH), f32),
            pltpu.SemaphoreType.DMA((4,)),
        ],
    )
    got_one = pair_swap(send)
    sent, grown = call(
        first_merge_kernel,
        (
            jax.ShapeDtypeStruct((8 * chips, DH), f32),
            jax.ShapeDtypeStruct((8, DH), f32),
        ),
        mine_one,
        got_one,
        place=core,
        scratch_shapes=[pltpu.VMEM((DH, DH), f32)],
    )

    first_got = exchanged(sent)

    sums = jax.ShapeDtypeStruct(decay_one.shape, f32)
    within_one, within_two, late_grad = call(
        decay_kernel,
        (sums, sums, jax.ShapeDtypeStruct(grad_out.shape, bf16)),
        decay_one,
        decay_two,
        grad_out,
        after=(sent,),
    )
    end_one, end_two = within_one[:, -1:], within_two[:, -1:]
    first_one, first_two = call(
        pick_kernel, (flat,) * 2, initial_one, initial_two, place=core, after=(within_one,)
    )
    grow_one, _ = grow_tail(within_one, end_one)
    grow_two, tail_two = grow_tail(within_two, end_two)
    weights_one = (mm("hcd,hsd->hcs", query_one, key_one) * causal_exp(within_one)).astype(bf16)
    inner_one = mm("hcs,hse->hce", weights_one, value_one)
    weights_two = (mm("hcd,hsd->hcs", query_two, key_two) * causal_exp(within_two)).astype(bf16)
    keys_scaled_two = (key_two * tail_two).astype(bf16)
    queries_scaled_two = (query_two * grow_two).astype(bf16)
    queries_scaled_one = (query_one * grow_one).astype(bf16)

    matrix = jax.ShapeDtypeStruct((4 * chips, 4 * chips), bf16)
    back, start, *matrices = call(
        first_scan_kernel,
        (flat, jax.ShapeDtypeStruct((8, DH), f32)) + (matrix,) * 6,
        first_got,
        place=place,
        after=(
            inner_one,
            weights_two,
            keys_scaled_two,
            queries_scaled_two,
            queries_scaled_one,
            first_one,
        ),
    )
    states_one = entering(0, exchanged(back), mine_one, got_one, first_one)
    output_one = inner_one + grow_one * mm("hcd,hde->hce", query_one, states_one)
    squares_one = head_sum(jnp.sum(output_one * output_one, axis=(0, 2))[None])[0]
    factor_one = lax.rsqrt(squares_one / features + 1e-06)
    normal_one = output_one * factor_one[None, :, None]
    value_two = normal_one.astype(bf16)

    mine, got = halves(mm("hsd,hse->hde", keys_scaled_two, value_two))
    state = scanned(matrices[:2], merged(3, True, mine, got))
    states_two = entering(1, state, mine, got, first_two)
    inner_two = mm("hcs,hse->hce", later(state, weights_two), value_two)
    output_two = inner_two + grow_two * mm("hcd,hde->hce", query_two, states_two)
    cotangent_two = late_grad.astype(jnp.float32)
    sums = head_sum(
        jnp.stack(
            [
                jnp.sum(output_two * output_two, axis=(0, 2)),
                jnp.sum(output_two * cotangent_two, axis=(0, 2)),
            ]
        )
    )
    factor_two = lax.rsqrt(sums[0] / features + 1e-06)
    inner_sum_two = factor_two * sums[1] / features

    def grad_core_of(cotangent, normalized, factor, inner_sum):
        core = factor[None, :, None] * (cotangent - normalized * inner_sum[None, :, None])
        return lax.optimization_barrier(core.astype(bf16))

    normal_two = output_two * factor_two[None, :, None]
    result = normal_two.astype(bf16)

    core_two = grad_core_of(cotangent_two, normal_two, factor_two, inner_sum_two)
    mine, got = halves(mm("hcd,hce->hde", queries_scaled_two, core_two))
    grad = scanned(matrices[2:4], merged(2, False, mine, got))
    grads_two = placed(*left(3, grad, mine, got))
    local_value_two = mm("hcs,hce->hse", later(grad, weights_two), core_two)
    grad_value_two = (
        local_value_two + tail_two * mm("hsd,hde->hse", key_two, grads_two)
    ).astype(bf16)

    cotangent_one = grad_value_two.astype(jnp.float32)
    inner_sum_one = head_sum(jnp.sum(cotangent_one * normal_one, axis=(0, 2))[None])[0] / features
    core_one = grad_core_of(cotangent_one, normal_one, factor_one, inner_sum_one)
    mine, got = halves(mm("hcd,hce->hde", queries_scaled_one, core_one))
    total = merged(0, False, mine, got)

    def query_grad(core_grad, values, within, end, keys, states):
        grow, tail = grow_tail(within, end)
        scores = (mm("hce,hse->hcs", core_grad, values) * causal_exp(within)).astype(bf16)
        grad_query = mm("hcs,hsd->hcd", scores, keys) + grow * mm(
            "hce,hde->hcd", core_grad, states
        )
        return scores, grad_query.astype(bf16), tail

    last_got = exchanged(total)
    last_one, last_two, last_end_one, last_end_two, last_weights, last_key, last_value, result = later(
        total,
        within_one,
        within_two,
        end_one,
        end_two,
        weights_one,
        key_one,
        value_one,
        result,
    )
    scores_two, grad_query_two, last_tail = query_grad(
        core_two, value_two, last_two, last_end_two, key_two, states_two
    )
    grad_key_two = (
        mm("hcs,hcd->hsd", scores_two, query_two)
        + last_tail * mm("hse,hde->hsd", value_two, grads_two)
    ).astype(bf16)
    scores_one, grad_query_one, last_tail = query_grad(
        core_one, value_one, last_one, last_end_one, key_one, states_one
    )
    local_key_one = mm("hcs,hcd->hsd", scores_one, query_one)
    local_value_one = mm("hcs,hce->hse", last_weights, core_one)
    last_tail = jnp.broadcast_to(last_tail, local_key_one.shape)
    back = call(
        scan_kernel,
        flat,
        *matrices[4:],
        last_got,
        after=(
            grad_query_two,
            grad_key_two,
            grad_query_one,
            local_key_one,
            local_value_one,
            last_tail,
        ),
    )
    keep, send = left(1, exchanged(back), mine, got)
    grad_key_one, grad_value_one = call(
        last_kernel,
        (jax.ShapeDtypeStruct(key_one.shape, bf16),) * 2,
        keep,
        pair_swap(send),
        last_key,
        last_value,
        last_tail,
        local_key_one,
        local_value_one,
        place=core,
    )
    return result, grad_query_one, grad_key_one, grad_value_one, grad_query_two, grad_key_two


def solution(mesh):
    seq = ("chip", "core")
    finer = Mesh(
        mesh.devices.reshape(mesh.shape["seq"] // 2, 2, mesh.shape["head"]), seq + ("head",)
    )
    tokens = P("head", seq, None)
    decay = P("head", seq)
    state = P("head", None, None)
    return jax.shard_map(
        local,
        mesh=finer,
        in_specs=(
            tokens,
            tokens,
            tokens,
            decay,
            state,
            tokens,
            tokens,
            decay,
            state,
            tokens,
        ),
        out_specs=(tokens,) * 6,
        check_vma=False,
    )
```

time: 173 us -> 167 us (0.965)
  blocking collectives: 0 us -> 72.9 us
  waiting for transfers between devices: 84.5 us -> 32.1 us
  starting transfers between devices: 60.9 us -> 45.1 us
  matrix products: 14 us -> 5.23 us
  local copies, waits for them, and re-layouts: 9.71 us -> 2.55 us
  Pallas kernels: 0.03 us -> 6.53 us
    all_to_all x0 -> x6, blocking collectives: none -> 72.9 us  [swap(): lax.all_to_all(pieces, 'chip', split_axis=0, concat_axis=0, tiled=True)]
    all_to_all x8 -> x2, waiting for transfers between devices: 75.6 us -> 15.7 us  [swap(): lax.all_to_all(pieces, 'chip', split_axis=0, concat_axis=0, tiled=True)]
    all_to_all x8 -> x2, starting transfers between devices: 52.8 us -> 13.5 us  [swap(): lax.all_to_all(pieces, 'chip', split_axis=0, concat_axis=0, tiled=True)]
    ppermute x9 -> x14, starting transfers between devices: 8.07 us -> 31.6 us  [the longest x8 22.6 us: pair_swap(): return lax.ppermute(values, 'core', ((0, 1), (1, 0)))]
    ppermute x9 -> x14, waiting for transfers between devices: 8.88 us -> 16.4 us  [the longest x6 9.52 us: head_sum(): total = total + lax.ppermute(total, 'head', both)]
    dot_general x24 -> x21, matrix products: 12.3 us -> 5.23 us  [mm(): return jnp.einsum(spec, a, b, preferred_element_type=jnp.float32)]
    pallas_call x4 -> x25, Pallas kernels: 0.03 us -> 6.53 us  [call(): pl.pallas_call(kernel, out_shape=out_shape, in_specs=specs, compiler_para...]
    all_to_all x5 -> x0, local copies, waits for them, and re-layouts: 3.94 us -> none  [swap(): lax.all_to_all(pieces, 'seq', split_axis=0, concat_axis=0, tiled=True)]
  transfers between devices with their start and end apart: 17 -> 16, of which waited for: 15 -> 16; matrix products, arithmetic and copies ran while one was open for 4% -> 1% of each run, Pallas kernels for 0% -> 0%
where the time goes in v2:
time: 167 us
  blocking collectives  72.9 us (44%)
  starting transfers between devices  45.1 us (27%)
  waiting for transfers between devices  32.1 us (19%)
  Pallas kernels  6.53 us (4%)
  matrix products  5.23 us (3%)
  local copies, waits for them, and re-layouts  2.55 us (2%)
    all_to_all x6, blocking collectives, swap(): lax.all_to_all(pieces, 'chip', split_axis=0, concat_axis=0, tiled=True)  72.9 us
    ppermute x8, starting transfers between devices, pair_swap(): return lax.ppermute(values, 'core', ((0, 1), (1, 0)))  22.6 us
    all_to_all x2, waiting for transfers between devices, swap(): lax.all_to_all(pieces, 'chip', split_axis=0, concat_axis=0, tiled=True)  15.7 us
    all_to_all x2, starting transfers between devices, swap(): lax.all_to_all(pieces, 'chip', split_axis=0, concat_axis=0, tiled=True)  13.5 us
    ppermute x6, waiting for transfers between devices, head_sum(): total = total + lax.ppermute(total, 'head', both)  9.52 us
    ppermute x6, starting transfers between devices, head_sum(): total = total + lax.ppermute(total, 'head', both)  9.01 us
    ppermute x8, waiting for transfers between devices, pair_swap(): return lax.ppermute(values, 'core', ((0, 1), (1, 0)))  6.87 us
    pallas_call x25, Pallas kernels, call(): pl.pallas_call(kernel, out_shape=out_shape, in_specs=specs, compiler_para...  6.53 us
  transfers between devices with their start and end apart: 16, of which 16 were waited for; matrix products, arithmetic and copies ran while one was open for 1% of the time, Pallas kernels for 0%

profile of v2, /device:TPU:1, one launch (start us, length us, event | category | flops | bytes accessed | tf_op | source)
XLA Modules:
  0.0 166.6 jit_solution(13852256802637144890)
XLA Ops:
  0.6 2.1 %shard_map.145 = (f32[136,128]{1,0:T(8,128)}, f32[136,128]{1,0:T(8,128)}) custom-call(s32[1]{0:T(128)} %bitcast.core_ref.refs_0_, bf16[2,256,128]{2,1,0:T(8,128)(2,1)} %refs_5_.1, bf16[2,256,128]{2,1,0:T(8,128)(2,1)} %refs_6_.1, f32[2,256]{1,0:T(2,128)} %refs_0_.1, f32[2,256]{1,0:T(2,128)} %refs_1_.2), custom_call_target="tpu_custom_call" | custom-call | tf_op jit(solution)/shard_map/pallas_call | solution.py:51
  2.7 3.3 %collective-permute-start = (f32[136,128]{1,0:T(8,128)}, f32[136,128]{1,0:T(8,128)S(1)}, u32[]{:S(2)}, u32[]{:S(2)}) collective-permute-start(f32[136,128]{1,0:T(8,128)} %get-tuple-element.48), channel_id=1, source_target_pairs={{0,4},{4,0},{1,5},{5,1},{2,6},{6,2},{3,7},{7,3},{8,12},{12,8},{9,1... | collective-permute-start | bytes 208904 | tf_op jit(solution)/shard_map/ppermute | solution.py:35
  6.0 1.1 collective-permute-done.got_ref
  10.0 9.6 %all-to-all-start = ((f32[32,8,128]{2,1,0:T(8,128)}), f32[32,8,128]{2,1,0:T(8,128)S(1)}, u32[]{:S(2)}, u32[]{:S(2)}) async-start(f32[32,8,128]{2,1,0:T(8,128)} %bitcast.2), calls=%async_computation | async-start | bytes 262144 | tf_op jit(solution)/shard_map/all_to_all | solution.py:31
  21.3 7.5 %all-to-all-done = f32[32,8,128]{2,1,0:T(8,128)S(1)} async-done(((f32[32,8,128]{2,1,0:T(8,128)}), f32[32,8,128]{2,1,0:T(8,128)S(1)}, u32[]{:S(2)}, u32[]{:S(2)}) %all-to-all-start) | async-done | bytes 131104 | tf_op jit(solution)/shard_map/all_to_all | solution.py:31
  29.4 13.1 %all_to_all.40 = f32[32,4,128]{2,1,0:T(4,128)S(1)} all-to-all(f32[32,4,128]{2,1,0:T(4,128)S(1)} %bitcast.99), channel_id=1, replica_groups=mesh['chip'=32,'core'=2,'head'=4] {'chip'}, dimensions={0} | all-to-all | bytes 131072 | tf_op jit(solution)/shard_map/all_to_all | solution.py:31
  42.5 2.6 %collective-permute-start.1 = (f32[128,128]{1,0:T(8,128)S(1)}, f32[128,128]{1,0:T(8,128)S(1)}, u32[]{:S(2)}, u32[]{:S(2)}) collective-permute-start(f32[128,128]{1,0:T(8,128)S(1)} %get-tuple-element.59), channel_id=1, source_target_pairs={{0,4},{4,0},{1,5},{5,1},{2,6},{6,2},{3,7},{7,3},{8,12},{12,8},{9,1... | collective-permute-start | bytes 196616 | tf_op jit(solution)/shard_map/ppermute | solution.py:35
  46.3 1.3 collective-permute-start.2
  47.6 1.2 collective-permute-done.2
  48.9 2.5 %collective-permute-start.3 = (f32[1,256]{1,0:T(1,128)S(1)}, f32[1,256]{1,0:T(1,128)S(1)}, u32[]{:S(2)}, u32[]{:S(2)}) collective-permute-start(f32[1,256]{1,0:T(1,128)S(1)} %add.56), channel_id=1, source_target_pairs={{1,2},{2,1},{3,0},{0,3},{5,6},{6,5},{7,4},{4,7},{9,10},{10,9},{11,... | collective-permute-start | bytes 3080 | tf_op jit(solution)/shard_map/ppermute | solution.py:18
  51.3 1.2 collective-permute-done.3
  52.8 2.7 %collective-permute-start.4 = (f32[128,128]{1,0:T(8,128)S(1)}, f32[128,128]{1,0:T(8,128)S(1)}, u32[]{:S(2)}, u32[]{:S(2)}) collective-permute-start(f32[128,128]{1,0:T(8,128)S(1)} %get-tuple-element.61), channel_id=1, source_target_pairs={{0,4},{4,0},{1,5},{5,1},{2,6},{6,2},{3,7},{7,3},{8,12},{12,8},{9,1... | collective-permute-start | bytes 196616 | tf_op jit(solution)/shard_map/ppermute | solution.py:35
  56.4 11.9 %all_to_all.41 = f32[32,4,128]{2,1,0:T(4,128)S(1)} all-to-all(f32[32,4,128]{2,1,0:T(4,128)S(1)} %bitcast.95), channel_id=1, replica_groups=mesh['chip'=32,'core'=2,'head'=4] {'chip'}, dimensions={0} | all-to-all | bytes 131072 | tf_op jit(solution)/shard_map/all_to_all | solution.py:31
  68.5 12.0 %all_to_all.42 = f32[32,4,128]{2,1,0:T(4,128)S(1)} all-to-all(f32[32,4,128]{2,1,0:T(4,128)S(1)} %bitcast.92), channel_id=1, replica_groups=mesh['chip'=32,'core'=2,'head'=4] {'chip'}, dimensions={0} | all-to-all | bytes 131072 | tf_op jit(solution)/shard_map/all_to_all | solution.py:31
  80.5 3.0 %collective-permute-start.5 = (f32[128,128]{1,0:T(8,128)S(1)}, f32[128,128]{1,0:T(8,128)S(1)}, u32[]{:S(2)}, u32[]{:S(2)}) collective-permute-start(f32[128,128]{1,0:T(8,128)S(1)} %get-tuple-element.64), channel_id=1, source_target_pairs={{0,4},{4,0},{1,5},{5,1},{2,6},{6,2},{3,7},{7,3},{8,12},{12,8},{9,1... | collective-permute-start | bytes 196616 | tf_op jit(solution)/shard_map/ppermute | solution.py:35
  84.9 2.4 %collective-permute-done.6 = f32[2,256]{1,0:T(2,128)S(1)} collective-permute-done((f32[2,256]{1,0:T(2,128)S(1)}, f32[2,256]{1,0:T(2,128)S(1)}, u32[]{:S(2)}, u32[]{:S(2)}) %collective-permute-start.6) | collective-permute-done | bytes 2080 | tf_op jit(solution)/shard_map/ppermute | solution.py:18
  87.3 2.6 %collective-permute-start.7 = (f32[2,256]{1,0:T(2,128)S(1)}, f32[2,256]{1,0:T(2,128)S(1)}, u32[]{:S(2)}, u32[]{:S(2)}) collective-permute-start(f32[2,256]{1,0:T(2,128)S(1)} %fusion.19), channel_id=1, source_target_pairs={{1,2},{2,1},{3,0},{0,3},{5,6},{6,5},{7,4},{4,7},{9,10},{10,9},{11,... | collective-permute-start | bytes 6152 | tf_op jit(solution)/shard_map/ppermute | solution.py:18
  89.9 1.2 collective-permute-done.7
  91.5 2.7 %collective-permute-start.8 = (f32[128,128]{1,0:T(8,128)S(1)}, f32[128,128]{1,0:T(8,128)S(1)}, u32[]{:S(2)}, u32[]{:S(2)}) collective-permute-start(f32[128,128]{1,0:T(8,128)S(1)} %get-tuple-element.69), channel_id=1, source_target_pairs={{0,4},{4,0},{1,5},{5,1},{2,6},{6,2},{3,7},{7,3},{8,12},{12,8},{9,1... | collective-permute-start | bytes 196616 | tf_op jit(solution)/shard_map/ppermute | solution.py:35
  94.2 0.9 collective-permute-done.8.got_ref
  95.1 11.8 %all_to_all.43 = f32[32,4,128]{2,1,0:T(4,128)S(1)} all-to-all(f32[32,4,128]{2,1,0:T(4,128)S(1)} %bitcast.96), channel_id=1, replica_groups=mesh['chip'=32,'core'=2,'head'=4] {'chip'}, dimensions={0} | all-to-all | bytes 131072 | tf_op jit(solution)/shard_map/all_to_all | solution.py:31
  107.1 12.0 %all_to_all.44 = f32[32,4,128]{2,1,0:T(4,128)S(1)} all-to-all(f32[32,4,128]{2,1,0:T(4,128)S(1)} %bitcast.94), channel_id=1, replica_groups=mesh['chip'=32,'core'=2,'head'=4] {'chip'}, dimensions={0} | all-to-all | bytes 131072 | tf_op jit(solution)/shard_map/all_to_all | solution.py:31
  119.2 2.8 %collective-permute-start.9 = (f32[128,128]{1,0:T(8,128)S(1)}, f32[128,128]{1,0:T(8,128)S(1)}, u32[]{:S(2)}, u32[]{:S(2)}) collective-permute-start(f32[128,128]{1,0:T(8,128)S(1)} %get-tuple-element.71), channel_id=1, source_target_pairs={{0,4},{4,0},{1,5},{5,1},{2,6},{6,2},{3,7},{7,3},{8,12},{12,8},{9,1... | collective-permute-start | bytes 196616 | tf_op jit(solution)/shard_map/ppermute | solution.py:35
  123.3 2.4 %collective-permute-done.10 = f32[1,256]{1,0:T(1,128)S(1)} collective-permute-done((f32[1,256]{1,0:T(1,128)S(1)}, f32[1,256]{1,0:T(1,128)S(1)}, u32[]{:S(2)}, u32[]{:S(2)}) %collective-permute-start.10) | collective-permute-done | bytes 1056 | tf_op jit(solution)/shard_map/ppermute | solution.py:18
  125.7 2.5 %collective-permute-start.11 = (f32[1,256]{1,0:T(1,128)S(1)}, f32[1,256]{1,0:T(1,128)S(1)}, u32[]{:S(2)}, u32[]{:S(2)}) collective-permute-start(f32[1,256]{1,0:T(1,128)S(1)} %add.64), channel_id=1, source_target_pairs={{1,2},{2,1},{3,0},{0,3},{5,6},{6,5},{7,4},{4,7},{9,10},{10,9},{11,... | collective-permute-start | bytes 3080 | tf_op jit(solution)/shard_map/ppermute | solution.py:18
  128.2 1.2 collective-permute-done.11
  129.7 2.7 %collective-permute-start.12 = (f32[128,128]{1,0:T(8,128)S(1)}, f32[128,128]{1,0:T(8,128)S(1)}, u32[]{:S(2)}, u32[]{:S(2)}) collective-permute-start(f32[128,128]{1,0:T(8,128)S(1)} %get-tuple-element.73), channel_id=1, source_target_pairs={{0,4},{4,0},{1,5},{5,1},{2,6},{6,2},{3,7},{7,3},{8,12},{12,8},{9,1... | collective-permute-start | bytes 196616 | tf_op jit(solution)/shard_map/ppermute | solution.py:35
  136.9 3.9 %all-to-all-start.6 = ((f32[32,4,128]{2,1,0:T(4,128)}), f32[32,4,128]{2,1,0:T(4,128)S(1)}, u32[]{:S(2)}, u32[]{:S(2)}) async-start(f32[32,4,128]{2,1,0:T(4,128)} %bitcast.25), calls=%async_computation.6 | async-start | bytes 131072 | tf_op jit(solution)/shard_map/all_to_all | solution.py:31
  141.5 8.1 %all-to-all-done.6 = f32[32,4,128]{2,1,0:T(4,128)S(1)} async-done(((f32[32,4,128]{2,1,0:T(4,128)}), f32[32,4,128]{2,1,0:T(4,128)S(1)}, u32[]{:S(2)}, u32[]{:S(2)}) %all-to-all-start.6) | async-done | bytes 65568 | tf_op jit(solution)/shard_map/all_to_all | solution.py:31
  150.0 12.1 %all_to_all.45 = f32[32,4,128]{2,1,0:T(4,128)S(1)} all-to-all(f32[32,4,128]{2,1,0:T(4,128)S(1)} %bitcast.98), channel_id=1, replica_groups=mesh['chip'=32,'core'=2,'head'=4] {'chip'}, dimensions={0} | all-to-all | bytes 131072 | tf_op jit(solution)/shard_map/all_to_all | solution.py:31
  162.1 2.7 %collective-permute-start.13 = (f32[128,128]{1,0:T(8,128)S(1)}, f32[128,128]{1,0:T(8,128)S(1)}, u32[]{:S(2)}, u32[]{:S(2)}) collective-permute-start(f32[128,128]{1,0:T(8,128)S(1)} %get-tuple-element.83), channel_id=1, source_target_pairs={{0,4},{4,0},{1,5},{5,1},{2,6},{6,2},{3,7},{7,3},{8,12},{12,8},{9,1... | collective-permute-start | bytes 196616 | tf_op jit(solution)/shard_map/ppermute | solution.py:35
  165.6 0.9 shard_map.169
  (105 shorter events, 17.5 us)
Async XLA Ops:
  2.7 4.4 %copy-start.5 = (f32[136,128]{1,0:T(8,128)S(1)}, f32[136,128]{1,0:T(8,128)}, u32[]{:S(2)}) copy-start(f32[136,128]{1,0:T(8,128)} %get-tuple-element.47.mine_ref) | copy-start | bytes 208900
  2.7 5.2 %copy-start.6 = (bf16[2,256,128]{2,1,0:T(8,128)(2,1)S(1)}, bf16[2,256,128]{2,1,0:T(8,128)(2,1)}, u32[]{:S(2)}) copy-start(bf16[2,256,128]{2,1,0:T(8,128)(2,1)} %refs_2_.2) | copy-start | bytes 393220
  2.7 4.4 %collective-permute-start = (f32[136,128]{1,0:T(8,128)}, f32[136,128]{1,0:T(8,128)S(1)}, u32[]{:S(2)}, u32[]{:S(2)}) collective-permute-start(f32[136,128]{1,0:T(8,128)} %get-tuple-element.48), channel_id=1, source_target_pairs={{0,4},{4,0},{1,5},{5,1},{2,6},{6,2},{3,7},{7,3},{8,12},{12,8},{9,1... | collective-permute-start | bytes 208904 | tf_op jit(solution)/shard_map/ppermute | solution.py:35
  7.1 0.8 copy-start.9
  7.1 0.8 copy-start.10
  7.9 0.9 copy-start.1
  7.9 1.0 copy-start.12
  8.9 0.9 copy-start
  10.0 9.7 %copy-start.11 = (bf16[2,256,128]{2,1,0:T(8,128)(2,1)S(1)}, bf16[2,256,128]{2,1,0:T(8,128)(2,1)}, u32[]{:S(2)}) copy-start(bf16[2,256,128]{2,1,0:T(8,128)(2,1)} %param.16) | copy-start | bytes 393220
  10.0 9.7 %copy-start.13 = (bf16[2,256,128]{2,1,0:T(8,128)(2,1)S(1)}, bf16[2,256,128]{2,1,0:T(8,128)(2,1)}, u32[]{:S(2)}) copy-start(bf16[2,256,128]{2,1,0:T(8,128)(2,1)} %param.15) | copy-start | bytes 393220
  10.0 18.8 %all-to-all-start = ((f32[32,8,128]{2,1,0:T(8,128)}), f32[32,8,128]{2,1,0:T(8,128)S(1)}, u32[]{:S(2)}, u32[]{:S(2)}) async-start(f32[32,8,128]{2,1,0:T(8,128)} %bitcast.2), calls=%async_computation | async-start | bytes 262144 | tf_op jit(solution)/shard_map/all_to_all | solution.py:31
  20.1 0.9 copy-start.7
  20.1 1.0 copy-start.8
  42.5 3.5 %collective-permute-start.1 = (f32[128,128]{1,0:T(8,128)S(1)}, f32[128,128]{1,0:T(8,128)S(1)}, u32[]{:S(2)}, u32[]{:S(2)}) collective-permute-start(f32[128,128]{1,0:T(8,128)S(1)} %get-tuple-element.59), channel_id=1, source_target_pairs={{0,4},{4,0},{1,5},{5,1},{2,6},{6,2},{3,7},{7,3},{8,12},{12,8},{9,1... | collective-permute-start | bytes 196616 | tf_op jit(solution)/shard_map/ppermute | solution.py:35
  46.3 2.5 %collective-permute-start.2 = (f32[1,256]{1,0:T(1,128)S(1)}, f32[1,256]{1,0:T(1,128)S(1)}, u32[]{:S(2)}, u32[]{:S(2)}) collective-permute-start(f32[1,256]{1,0:T(1,128)S(1)} %bitcast.111), channel_id=1, source_target_pairs={{0,1},{1,0},{2,3},{3,2},{4,5},{5,4},{6,7},{7,6},{8,9},{9,8},{10,11... | collective-permute-start | bytes 3080 | tf_op jit(solution)/shard_map/ppermute | solution.py:18
  48.9 3.6 %collective-permute-start.3 = (f32[1,256]{1,0:T(1,128)S(1)}, f32[1,256]{1,0:T(1,128)S(1)}, u32[]{:S(2)}, u32[]{:S(2)}) collective-permute-start(f32[1,256]{1,0:T(1,128)S(1)} %add.56), channel_id=1, source_target_pairs={{1,2},{2,1},{3,0},{0,3},{5,6},{6,5},{7,4},{4,7},{9,10},{10,9},{11,... | collective-permute-start | bytes 3080 | tf_op jit(solution)/shard_map/ppermute | solution.py:18
  52.8 3.6 %collective-permute-start.4 = (f32[128,128]{1,0:T(8,128)S(1)}, f32[128,128]{1,0:T(8,128)S(1)}, u32[]{:S(2)}, u32[]{:S(2)}) collective-permute-start(f32[128,128]{1,0:T(8,128)S(1)} %get-tuple-element.61), channel_id=1, source_target_pairs={{0,4},{4,0},{1,5},{5,1},{2,6},{6,2},{3,7},{7,3},{8,12},{12,8},{9,1... | collective-permute-start | bytes 196616 | tf_op jit(solution)/shard_map/ppermute | solution.py:35
  80.5 3.9 %collective-permute-start.5 = (f32[128,128]{1,0:T(8,128)S(1)}, f32[128,128]{1,0:T(8,128)S(1)}, u32[]{:S(2)}, u32[]{:S(2)}) collective-permute-start(f32[128,128]{1,0:T(8,128)S(1)} %get-tuple-element.64), channel_id=1, source_target_pairs={{0,4},{4,0},{1,5},{5,1},{2,6},{6,2},{3,7},{7,3},{8,12},{12,8},{9,1... | collective-permute-start | bytes 196616 | tf_op jit(solution)/shard_map/ppermute | solution.py:35
  84.8 2.5 %collective-permute-start.6 = (f32[2,256]{1,0:T(2,128)S(1)}, f32[2,256]{1,0:T(2,128)S(1)}, u32[]{:S(2)}, u32[]{:S(2)}) collective-permute-start(f32[2,256]{1,0:T(2,128)S(1)} %pad_maximum_fusion), channel_id=1, source_target_pairs={{0,1},{1,0},{2,3},{3,2},{4,5},{5,4},{6,7},{7,6},{8,9},{9,8},{10,11... | collective-permute-start | bytes 6152 | tf_op jit(solution)/shard_map/ppermute | solution.py:18
  87.3 3.7 %collective-permute-start.7 = (f32[2,256]{1,0:T(2,128)S(1)}, f32[2,256]{1,0:T(2,128)S(1)}, u32[]{:S(2)}, u32[]{:S(2)}) collective-permute-start(f32[2,256]{1,0:T(2,128)S(1)} %fusion.19), channel_id=1, source_target_pairs={{1,2},{2,1},{3,0},{0,3},{5,6},{6,5},{7,4},{4,7},{9,10},{10,9},{11,... | collective-permute-start | bytes 6152 | tf_op jit(solution)/shard_map/ppermute | solution.py:18
  91.5 3.6 %collective-permute-start.8 = (f32[128,128]{1,0:T(8,128)S(1)}, f32[128,128]{1,0:T(8,128)S(1)}, u32[]{:S(2)}, u32[]{:S(2)}) collective-permute-start(f32[128,128]{1,0:T(8,128)S(1)} %get-tuple-element.69), channel_id=1, source_target_pairs={{0,4},{4,0},{1,5},{5,1},{2,6},{6,2},{3,7},{7,3},{8,12},{12,8},{9,1... | collective-permute-start | bytes 196616 | tf_op jit(solution)/shard_map/ppermute | solution.py:35
  119.2 3.7 %collective-permute-start.9 = (f32[128,128]{1,0:T(8,128)S(1)}, f32[128,128]{1,0:T(8,128)S(1)}, u32[]{:S(2)}, u32[]{:S(2)}) collective-permute-start(f32[128,128]{1,0:T(8,128)S(1)} %get-tuple-element.71), channel_id=1, source_target_pairs={{0,4},{4,0},{1,5},{5,1},{2,6},{6,2},{3,7},{7,3},{8,12},{12,8},{9,1... | collective-permute-start | bytes 196616 | tf_op jit(solution)/shard_map/ppermute | solution.py:35
  123.2 2.5 %collective-permute-start.10 = (f32[1,256]{1,0:T(1,128)S(1)}, f32[1,256]{1,0:T(1,128)S(1)}, u32[]{:S(2)}, u32[]{:S(2)}) collective-permute-start(f32[1,256]{1,0:T(1,128)S(1)} %bitcast.115), channel_id=1, source_target_pairs={{0,1},{1,0},{2,3},{3,2},{4,5},{5,4},{6,7},{7,6},{8,9},{9,8},{10,11... | collective-permute-start | bytes 3080 | tf_op jit(solution)/shard_map/ppermute | solution.py:18
  125.7 3.6 %collective-permute-start.11 = (f32[1,256]{1,0:T(1,128)S(1)}, f32[1,256]{1,0:T(1,128)S(1)}, u32[]{:S(2)}, u32[]{:S(2)}) collective-permute-start(f32[1,256]{1,0:T(1,128)S(1)} %add.64), channel_id=1, source_target_pairs={{1,2},{2,1},{3,0},{0,3},{5,6},{6,5},{7,4},{4,7},{9,10},{10,9},{11,... | collective-permute-start | bytes 3080 | tf_op jit(solution)/shard_map/ppermute | solution.py:18
  129.7 3.6 %collective-permute-start.12 = (f32[128,128]{1,0:T(8,128)S(1)}, f32[128,128]{1,0:T(8,128)S(1)}, u32[]{:S(2)}, u32[]{:S(2)}) collective-permute-start(f32[128,128]{1,0:T(8,128)S(1)} %get-tuple-element.73), channel_id=1, source_target_pairs={{0,4},{4,0},{1,5},{5,1},{2,6},{6,2},{3,7},{7,3},{8,12},{12,8},{9,1... | collective-permute-start | bytes 196616 | tf_op jit(solution)/shard_map/ppermute | solution.py:35
  136.9 12.8 %all-to-all-start.6 = ((f32[32,4,128]{2,1,0:T(4,128)}), f32[32,4,128]{2,1,0:T(4,128)S(1)}, u32[]{:S(2)}, u32[]{:S(2)}) async-start(f32[32,4,128]{2,1,0:T(4,128)} %bitcast.25), calls=%async_computation.6 | async-start | bytes 131072 | tf_op jit(solution)/shard_map/all_to_all | solution.py:31
  141.0 8.7 %copy-start.2 = (bf16[2,256,128]{2,1,0:T(8,128)(2,1)}, bf16[2,256,128]{2,1,0:T(8,128)(2,1)S(1)}, u32[]{:S(2)}) copy-start(bf16[2,256,128]{2,1,0:T(8,128)(2,1)S(1)} %fusion.13.refs_4_) | copy-start | bytes 393220
  141.3 8.5 %copy-start.3 = (bf16[2,256,128]{2,1,0:T(8,128)(2,1)}, bf16[2,256,128]{2,1,0:T(8,128)(2,1)S(1)}, u32[]{:S(2)}) copy-start(bf16[2,256,128]{2,1,0:T(8,128)(2,1)S(1)} %add_convert_fusion.refs_3_) | copy-start | bytes 393220
  141.5 8.3 %copy-start.4 = (bf16[2,256,128]{2,1,0:T(8,128)(2,1)}, bf16[2,256,128]{2,1,0:T(8,128)(2,1)S(1)}, u32[]{:S(2)}) copy-start(bf16[2,256,128]{2,1,0:T(8,128)(2,1)S(1)} %add_convert_fusion.1.refs_5_) | copy-start | bytes 393220
  162.1 3.6 %collective-permute-start.13 = (f32[128,128]{1,0:T(8,128)S(1)}, f32[128,128]{1,0:T(8,128)S(1)}, u32[]{:S(2)}, u32[]{:S(2)}) collective-permute-start(f32[128,128]{1,0:T(8,128)S(1)} %get-tuple-element.83), channel_id=1, source_target_pairs={{0,4},{4,0},{1,5},{5,1},{2,6},{6,2},{3,7},{7,3},{8,12},{12,8},{9,1... | collective-permute-start | bytes 196616 | tf_op jit(solution)/shard_map/ppermute | solution.py:35
